TPU v7x, 32 devices: a whole 2x2x4 slice. The times are simulated.
32 devices in a mesh: dp: 8 (over z, core), tensor: 4 (over y, x).
Axes of the slice: x: 2, y: 2, z: 4, core: 2. Of those that a mesh axis runs over, the one named last changes fastest.
Arguments:
- tokens: bfloat16 [65536, 1024], P(('dp', 'tensor')), may hold values from -6 to 6
- cotangent: bfloat16 [65536, 1024], P(('dp', 'tensor')), may hold values from -6 to 6
- clip_counts: int32 [8], P('dp'), may hold values from 1 to 8, as said below
- norm_params: float32 [6, 1024], replicated, as said below
- head_bias: float32 [2, 1024], replicated, may hold values from -1.75 to 1.75
- up_bias: float32 [4096], replicated, may hold values from -1.75 to 1.75
- w_qkv: float32 [1024, 3, 1024], P(None, None, 'tensor'), may hold values from -0.1875 to 0.1875
- w_out: float32 [1024, 1024], P('tensor'), may hold values from -0.75 to 0.75
- w_up: float32 [1024, 4096], P(None, 'tensor'), may hold values from -0.1875 to 0.1875
- w_down: float32 [4096, 1024], P('tensor'), may hold values from -0.125 to 0.125
- mom_norm: float32 [6, 1024], replicated, may hold values from -128 to 128
- mom_head_bias: float32 [2, 1024], replicated, may hold values from -128 to 128
- mom_up_bias: float32 [4096], replicated, may hold values from -128 to 128
- mom_qkv: float32 [1024, 3, 1024], P(None, None, 'tensor'), may hold values from -128 to 128
- mom_out: float32 [1024, 1024], P('tensor'), may hold values from -128 to 128
- mom_up: float32 [1024, 4096], P(None, 'tensor'), may hold values from -128 to 128
- mom_down: float32 [4096, 1024], P('tensor'), may hold values from -128 to 128
- err_qkv: float32 [8, 1024, 3, 1024], P('dp', None, None, 'tensor'), may hold values from -128 to 128
- err_out: float32 [8, 1024, 1024], P('dp', 'tensor'), may hold values from -128 to 128
- err_up: float32 [8, 1024, 4096], P('dp', None, 'tensor'), may hold values from -128 to 128
- err_down: float32 [8, 4096, 1024], P('dp', 'tensor'), may hold values from -128 to 128
- basis_qkv: float32 [4, 768, 8], P('tensor'), may hold values from -6 to 6
- basis_out: float32 [4, 1024, 8], P('tensor'), may hold values from -6 to 6
- basis_up: float32 [4, 1024, 8], P('tensor'), may hold values from -6 to 6
- basis_down: float32 [4, 1024, 8], P('tensor'), may hold values from -6 to 6
Outputs:
- block_out: bfloat16 [65536, 1024], P(('dp', 'tensor'))
- input_grad: bfloat16 [65536, 1024], P(('dp', 'tensor'))
- new_norm_params: float32 [6, 1024], replicated
- new_head_bias: float32 [2, 1024], replicated
- new_up_bias: float32 [4096], replicated
- new_w_qkv: float32 [1024, 3, 1024], P(None, None, 'tensor')
- new_w_out: float32 [1024, 1024], P('tensor')
- new_w_up: float32 [1024, 4096], P(None, 'tensor')
- new_w_down: float32 [4096, 1024], P('tensor')
- new_mom_norm: float32 [6, 1024], replicated
- new_mom_head_bias: float32 [2, 1024], replicated
- new_mom_up_bias: float32 [4096], replicated
- new_mom_qkv: float32 [1024, 3, 1024], P(None, None, 'tensor')
- new_mom_out: float32 [1024, 1024], P('tensor')
- new_mom_up: float32 [1024, 4096], P(None, 'tensor')
- new_mom_down: float32 [4096, 1024], P('tensor')
- new_err_qkv: float32 [8, 1024, 3, 1024], P('dp', None, None, 'tensor')
- new_err_out: float32 [8, 1024, 1024], P('dp', 'tensor')
- new_err_up: float32 [8, 1024, 4096], P('dp', None, 'tensor')
- new_err_down: float32 [8, 4096, 1024], P('dp', 'tensor')
- new_p_qkv: float32 [4, 1024, 8], P('tensor')
- new_p_out: float32 [4, 256, 8], P('tensor')
- new_p_up: float32 [4, 1024, 8], P('tensor')
- new_p_down: float32 [4, 1024, 8], P('tensor')
- new_q_qkv: float32 [4, 768, 8], P('tensor')
- new_q_out: float32 [4, 1024, 8], P('tensor')
- new_q_up: float32 [4, 1024, 8], P('tensor')
- new_q_down: float32 [4, 1024, 8], P('tensor')
Inputs may be any that keep to these rules, and one draw needn't show every extreme that they name: `clip_counts`: the number of live clips of each data replica; in every draw some replica holds 8 live clips and some other holds 1. `norm_params`: rows 0 and 3 are gains near 1; rows 1, 2, 4 and 5 are shifts and biases.
All inputs are finite; a program needn't handle non-finite values.
Results may differ from a plain program's by a relative error of at most 0.03.
Values may be sent and summed in bfloat16 or wider, within the bound.
No kernel may reach another device: no remote copies, remote signals or barrier semaphores. Data moves between devices by JAX's collectives and lax.ppermute only.
A program may use at most 384 MiB of HBM per device.

v0:
```python
import jax
import jax.numpy as jnp
from jax import lax
from jax.sharding import PartitionSpec as P

HEAD_DIM = 64
CLIP_LEN = 1024


PRECISE = lax.Precision.HIGHEST
NORM_EPS = 1e-06
STEP_RATE = 0.001
VECTOR_RATE = 0.015
MOMENTUM_DECAY = 0.9


def layer_norm(values):
    centre = values - jnp.mean(values, axis=-1, keepdims=True)
    spread = jnp.mean(centre * centre, axis=-1, keepdims=True)
    inv_std = lax.rsqrt(spread + NORM_EPS)
    return (centre * inv_std, inv_std)


def norm_back(grad_norm, normed, inv_std):
    mean_grad = jnp.mean(grad_norm, axis=-1, keepdims=True)
    mean_cross = jnp.mean(grad_norm * normed, axis=-1, keepdims=True)
    return inv_std * (grad_norm - mean_grad - normed * mean_cross)


def inner_rows(left_mat, right_mat, precision=None):
    return lax.dot_general(
        left_mat,
        right_mat,
        (((0,), (0,)), ((), ())),
        precision=precision,
        preferred_element_type=jnp.float32,
    )


def times_trans(left_mat, right_mat, precision=None):
    return lax.dot_general(
        left_mat,
        right_mat,
        (((1,), (1,)), ((), ())),
        precision=precision,
        preferred_element_type=jnp.float32,
    )


def orthonormal(factor):
    columns = []
    for column_pos in range(factor.shape[-1]):
        vector = factor[..., column_pos]
        for column in columns:
            vector = vector - jnp.sum(column * vector, axis=-1, keepdims=True) * column
        vector = vector * lax.rsqrt(jnp.sum(vector * vector, axis=-1, keepdims=True) + 1e-12)
        columns.append(vector)
    return jnp.stack(columns, axis=-1)


def gelu_exact(pre_act):
    return jax.nn.gelu(pre_act, approximate=False)


def attention_forward(queries, key_vecs, val_vecs):
    clip_len = queries.shape[1]
    q_block = min(512, clip_len)
    scale_qk = queries.shape[-1] ** (-0.5)
    offsets = jnp.arange(clip_len // q_block, dtype=jnp.int32) * q_block

    def one_clip(operands):
        clip_q, clip_k, clip_v = operands

        def one_block(offset):
            q_piece = lax.dynamic_slice_in_dim(clip_q, offset, q_block, 0)
            scores = (
                jnp.einsum("qhd,khd->hqk", q_piece, clip_k, preferred_element_type=jnp.float32)
                * scale_qk
            )
            row_max = jnp.max(scores, axis=-1, keepdims=True)
            exp_scores = jnp.exp(scores - row_max)
            row_sum = jnp.sum(exp_scores, axis=-1, keepdims=True)
            attn_prob = (exp_scores / row_sum).astype(jnp.bfloat16)
            context = jnp.einsum(
                "hqk,khd->qhd", attn_prob, clip_v, preferred_element_type=jnp.float32
            )
            return (context.astype(jnp.bfloat16), (row_max + jnp.log(row_sum))[..., 0])

        context, log_sums = lax.map(one_block, offsets)
        return (context.reshape(clip_q.shape), log_sums)

    return lax.map(one_clip, (queries, key_vecs, val_vecs))


def attention_backward(queries, key_vecs, val_vecs, log_sums, grad_context):
    clip_len = queries.shape[1]
    q_block = min(512, clip_len)
    scale_qk = queries.shape[-1] ** (-0.5)
    offsets = jnp.arange(clip_len // q_block, dtype=jnp.int32) * q_block

    def one_clip(operands):
        clip_q, clip_k, clip_v, clip_lse, clip_grad = operands

        def one_block(running, inputs):
            offset, block_lse = inputs
            q_piece = lax.dynamic_slice_in_dim(clip_q, offset, q_block, 0)
            grad_piece = lax.dynamic_slice_in_dim(clip_grad, offset, q_block, 0)
            scores = (
                jnp.einsum("qhd,khd->hqk", q_piece, clip_k, preferred_element_type=jnp.float32)
                * scale_qk
            )
            attn_prob = jnp.exp(scores - block_lse[..., None])
            grad_prob = jnp.einsum(
                "qhd,khd->hqk", grad_piece, clip_v, preferred_element_type=jnp.float32
            )
            inner_sum = jnp.sum(attn_prob * grad_prob, axis=-1, keepdims=True)
            grad_scores = (attn_prob * (grad_prob - inner_sum)).astype(jnp.bfloat16)
            grad_q = (
                jnp.einsum("hqk,khd->qhd", grad_scores, clip_k, preferred_element_type=jnp.float32)
                * scale_qk
            )
            grad_k = (
                running[0]
                + jnp.einsum(
                    "hqk,qhd->khd", grad_scores, q_piece, preferred_element_type=jnp.float32
                )
                * scale_qk
            )
            grad_v = running[1] + jnp.einsum(
                "hqk,qhd->khd",
                attn_prob.astype(jnp.bfloat16),
                grad_piece,
                preferred_element_type=jnp.float32,
            )
            return ((grad_k, grad_v), grad_q)

        zero_keys = jnp.zeros(clip_k.shape, jnp.float32)
        (grad_k, grad_v), grad_q = lax.scan(one_block, (zero_keys, zero_keys), (offsets, clip_lse))
        return (grad_q.reshape(clip_q.shape), grad_k, grad_v)

    return lax.map(one_clip, (queries, key_vecs, val_vecs, log_sums, grad_context))


def shards(
    tokens,
    cotangent,
    clip_counts,
    norm_params,
    head_bias,
    up_bias,
    w_qkv,
    w_out,
    w_up,
    w_down,
    mom_norm,
    mom_head_bias,
    mom_up_bias,
    mom_qkv,
    mom_out,
    mom_up,
    mom_down,
    err_qkv,
    err_out,
    err_up,
    err_down,
    basis_qkv,
    basis_out,
    basis_up,
    basis_down,
):
    tensor_count = lax.axis_size("tensor")
    tensor_pos = lax.axis_index("tensor")
    replica_count = lax.axis_size("dp")
    local_rows, model_width = tokens.shape
    head_dim = HEAD_DIM
    width_loc = w_out.shape[0]
    hidden_loc = w_up.shape[1]
    heads_loc = width_loc // head_dim
    rep_rows = local_rows * tensor_count
    clip_len = CLIP_LEN
    clip_count = rep_rows // clip_len
    row_ids = tensor_pos * local_rows + jnp.arange(local_rows, dtype=jnp.int32)
    live_rows = (row_ids // clip_len < clip_counts[0]).astype(jnp.float32)
    grad_rows = (cotangent.astype(jnp.float32) * live_rows[:, None]).astype(jnp.bfloat16)
    inputs_f = tokens.astype(jnp.float32)
    normed_one, inv_one = layer_norm(inputs_f)
    ln_one = (normed_one * norm_params[0] + norm_params[1]).astype(jnp.bfloat16)
    gathered_one = lax.all_gather(ln_one, "tensor", axis=0, tiled=True)
    col_start = tensor_pos * width_loc
    bias_q = lax.dynamic_slice_in_dim(head_bias[0], col_start, width_loc)
    bias_v = lax.dynamic_slice_in_dim(head_bias[1], col_start, width_loc)
    bias_qkv = jnp.concatenate([bias_q, jnp.zeros_like(bias_q), bias_v])
    qkv_weight = w_qkv.reshape(model_width, 3 * width_loc).astype(jnp.bfloat16)
    qkv_rows = (
        jnp.dot(gathered_one, qkv_weight, preferred_element_type=jnp.float32) + bias_qkv
    ).astype(jnp.bfloat16)
    qkv_rows = qkv_rows.reshape(clip_count, clip_len, 3, heads_loc, head_dim)
    queries = qkv_rows[:, :, 0]
    key_vecs = qkv_rows[:, :, 1]
    val_vecs = qkv_rows[:, :, 2]
    context, log_sums = attention_forward(queries, key_vecs, val_vecs)
    context_rows = context.reshape(rep_rows, width_loc)
    out_weight = w_out.astype(jnp.bfloat16)
    attn_sum = lax.psum_scatter(
        jnp.dot(context_rows, out_weight, preferred_element_type=jnp.float32).astype(jnp.bfloat16),
        "tensor",
        scatter_dimension=0,
        tiled=True,
    ).astype(jnp.float32)
    resid_one = inputs_f + attn_sum + norm_params[2]
    normed_two, inv_two = layer_norm(resid_one)
    ln_two = (normed_two * norm_params[3] + norm_params[4]).astype(jnp.bfloat16)
    up_full, down_full = (
        lax.all_gather(w_up.astype(jnp.bfloat16), "tensor", axis=1, tiled=True),
        lax.all_gather(w_down.astype(jnp.bfloat16), "tensor", axis=0, tiled=True),
    )
    pre_act = jnp.dot(ln_two, up_full, preferred_element_type=jnp.float32) + up_bias
    hidden = gelu_exact(pre_act).astype(jnp.bfloat16)
    ffn_sum = jnp.dot(hidden, down_full, preferred_element_type=jnp.float32)
    block_out = (resid_one + ffn_sum + norm_params[5]).astype(jnp.bfloat16)
    grad_hidden = times_trans(grad_rows, down_full)
    gelu_pull = jax.vjp(gelu_exact, pre_act)[1]
    grad_pre = gelu_pull(grad_hidden)[0].astype(jnp.bfloat16)
    grad_up_bias = jnp.sum(grad_pre.astype(jnp.float32), axis=0)
    grad_ln_two = times_trans(grad_pre, up_full)
    weight_grads = lax.psum_scatter(
        jnp.concatenate(
            [inner_rows(hidden, grad_rows), inner_rows(grad_pre, ln_two)], axis=1
        ).astype(jnp.bfloat16),
        "tensor",
        scatter_dimension=0,
        tiled=True,
    ).astype(jnp.float32)
    grad_down = weight_grads[:, :model_width]
    grad_up = jnp.transpose(weight_grads[:, model_width:])
    grad_res_one = grad_rows.astype(jnp.float32) + norm_back(
        grad_ln_two * norm_params[3], normed_two, inv_two
    )
    gain_two_grad = jnp.sum(grad_ln_two * normed_two, axis=0)
    shift_two_grad = jnp.sum(grad_ln_two, axis=0)
    down_bias_grad = jnp.sum(grad_rows.astype(jnp.float32), axis=0)
    out_bias_grad = jnp.sum(grad_res_one, axis=0)
    grad_attn = grad_res_one.astype(jnp.bfloat16)
    grad_attn_all = lax.all_gather(grad_attn, "tensor", axis=0, tiled=True)
    grad_out_w = inner_rows(context_rows, grad_attn_all)
    grad_context = times_trans(grad_attn_all, out_weight).astype(jnp.bfloat16)
    grad_context = grad_context.reshape(clip_count, clip_len, heads_loc, head_dim)
    grad_q, grad_k, grad_v = attention_backward(queries, key_vecs, val_vecs, log_sums, grad_context)
    grad_qkv = (
        jnp.stack([grad_q, grad_k, grad_v], axis=2)
        .astype(jnp.bfloat16)
        .reshape(rep_rows, 3 * width_loc)
    )
    grad_qkv_w = inner_rows(gathered_one, grad_qkv)
    qkv_bias_part = jnp.sum(grad_qkv.astype(jnp.float32), axis=0).reshape(3, width_loc)
    grad_head_bias = lax.dynamic_update_slice_in_dim(
        jnp.zeros((2, model_width), jnp.float32),
        jnp.stack([qkv_bias_part[0], qkv_bias_part[2]]),
        col_start,
        1,
    )
    grad_ln_one = lax.psum_scatter(
        times_trans(grad_qkv, qkv_weight).astype(jnp.bfloat16),
        "tensor",
        scatter_dimension=0,
        tiled=True,
    ).astype(jnp.float32)
    grad_input = grad_res_one + norm_back(grad_ln_one * norm_params[0], normed_one, inv_one)
    input_grad = grad_input.astype(jnp.bfloat16)
    gain_one_grad = jnp.sum(grad_ln_one * normed_one, axis=0)
    shift_one_grad = jnp.sum(grad_ln_one, axis=0)
    grad_norm = jnp.stack(
        [
            gain_one_grad,
            shift_one_grad,
            out_bias_grad,
            gain_two_grad,
            shift_two_grad,
            down_bias_grad,
        ]
    )
    sum_norm, sum_head, sum_up = lax.psum(
        (grad_norm, grad_head_bias, grad_up_bias), ("dp", "tensor")
    )
    new_vecs = []
    new_vec_moms = []
    for param_now, moment_now, grad_sum in zip(
        (norm_params, head_bias, up_bias),
        (mom_norm, mom_head_bias, mom_up_bias),
        (sum_norm, sum_head, sum_up),
    ):
        moment_new = MOMENTUM_DECAY * moment_now + grad_sum / replica_count
        new_vec_moms.append(moment_new)
        new_vecs.append(param_now - VECTOR_RATE * moment_new)
    grads_local = (grad_qkv_w, grad_out_w, grad_up, grad_down)
    errors_local = (err_qkv.reshape(model_width, 3 * width_loc), err_out[0], err_up[0], err_down[0])
    factors_local = (basis_qkv[0], basis_out[0], basis_up[0], basis_down[0])
    merged = [grad_now + error_now for grad_now, error_now in zip(grads_local, errors_local)]
    lefts = [
        jnp.dot(matrix, factor, precision=PRECISE) for matrix, factor in zip(merged, factors_local)
    ]
    left_sums = (
        lax.psum(lefts[0].astype(jnp.bfloat16), "dp").astype(jnp.float32),
        lax.psum(lefts[1].astype(jnp.bfloat16), "dp").astype(jnp.float32),
        lax.psum(lefts[2].astype(jnp.bfloat16), "dp").astype(jnp.float32),
        lax.psum(lefts[3].astype(jnp.bfloat16), "dp").astype(jnp.float32),
    )
    orthos = [orthonormal(left_sum) for left_sum in left_sums]
    rights = [inner_rows(matrix, ortho_left, PRECISE) for matrix, ortho_left in zip(merged, orthos)]
    right_sums = (
        lax.psum(rights[0].astype(jnp.bfloat16), "dp").astype(jnp.float32),
        lax.psum(rights[1].astype(jnp.bfloat16), "dp").astype(jnp.float32),
        lax.psum(rights[2].astype(jnp.bfloat16), "dp").astype(jnp.float32),
        lax.psum(rights[3].astype(jnp.bfloat16), "dp").astype(jnp.float32),
    )
    right_means = [right_sum / replica_count for right_sum in right_sums]
    approxs = [
        times_trans(ortho_left, right_mean, PRECISE)
        for ortho_left, right_mean in zip(orthos, right_means)
    ]
    new_errs = [matrix - approx for matrix, approx in zip(merged, approxs)]
    natural_shapes = (
        (model_width, 3, width_loc),
        (width_loc, model_width),
        (model_width, hidden_loc),
        (hidden_loc, model_width),
    )
    weights = (w_qkv, w_out, w_up, w_down)
    moments = (mom_qkv, mom_out, mom_up, mom_down)
    new_weights = []
    new_moments = []
    new_errors = []
    for weight, moment, approx, new_err, shape_now in zip(
        weights, moments, approxs, new_errs, natural_shapes
    ):
        moment_new = MOMENTUM_DECAY * moment + approx.reshape(shape_now)
        new_moments.append(moment_new)
        new_weights.append(weight - STEP_RATE * moment_new)
        new_errors.append(new_err.reshape((1,) + shape_now))
    return (
        block_out,
        input_grad,
        new_vecs[0],
        new_vecs[1],
        new_vecs[2],
        new_weights[0],
        new_weights[1],
        new_weights[2],
        new_weights[3],
        new_vec_moms[0],
        new_vec_moms[1],
        new_vec_moms[2],
        new_moments[0],
        new_moments[1],
        new_moments[2],
        new_moments[3],
        new_errors[0],
        new_errors[1],
        new_errors[2],
        new_errors[3],
        orthos[0][None],
        orthos[1][None],
        orthos[2][None],
        orthos[3][None],
        right_means[0][None],
        right_means[1][None],
        right_means[2][None],
        right_means[3][None],
    )


def solution(mesh):
    in_specs = (
        P(("dp", "tensor"), None),
        P(("dp", "tensor"), None),
        P("dp"),
        P(),
        P(),
        P(),
        P(None, None, "tensor"),
        P("tensor", None),
        P(None, "tensor"),
        P("tensor", None),
        P(),
        P(),
        P(),
        P(None, None, "tensor"),
        P("tensor", None),
        P(None, "tensor"),
        P("tensor", None),
        P("dp", None, None, "tensor"),
        P("dp", "tensor", None),
        P("dp", None, "tensor"),
        P("dp", "tensor", None),
        P("tensor", None, None),
        P("tensor", None, None),
        P("tensor", None, None),
        P("tensor", None, None),
    )
    out_specs = (
        P(("dp", "tensor"), None),
        P(("dp", "tensor"), None),
        P(),
        P(),
        P(),
        P(None, None, "tensor"),
        P("tensor", None),
        P(None, "tensor"),
        P("tensor", None),
        P(),
        P(),
        P(),
        P(None, None, "tensor"),
        P("tensor", None),
        P(None, "tensor"),
        P("tensor", None),
        P("dp", None, None, "tensor"),
        P("dp", "tensor", None),
        P("dp", None, "tensor"),
        P("dp", "tensor", None),
        P("tensor", None, None),
        P("tensor", None, None),
        P("tensor", None, None),
        P("tensor", None, None),
        P("tensor", None, None),
        P("tensor", None, None),
        P("tensor", None, None),
        P("tensor", None, None),
    )
    return jax.shard_map(shards, mesh=mesh, in_specs=in_specs, out_specs=out_specs, check_vma=False)
```

profile of v0, /device:TPU:10, one launch (start us, length us, event | category | flops | bytes accessed | tf_op | source)
XLA Modules:
  0.0 2073.6 jit_solution(1023592268937992677)
XLA Ops:
  20.6 156.5 %all-gather.5.cloned.1.call-done = bf16[8192,1024]{1,0:T(8,128)(2,1)} async-done(((bf16[2048,1024]{1,0:T(8,128)(2,1)}), bf16[8192,1024]{1,0:T(8,128)(2,1)}) %all-gather.5.cloned.1.call-update) | async-done | bytes 16777232 | tf_op jit(solution)/shard_map/all_gather | solution.py:188
  177.1 20.1 add_convert_fusion.1
  197.2 16.4 copy.71
  213.6 12.1 copy.256
  241.8 168.8 %while.58 = (s32[]{:T(128)}, bf16[8,1024,4,64]{3,2,1,0:T(4,128)(2,1)}, f32[8,2,4,512]{3,2,1,0:T(4,128)}, bf16[8,1024,4,64]{1,3,2,0:T(8,128)(2,1)}, bf16[8,1024,4...) while((s32[]{:T(128)}, ...), condition=%wide.region_7.8_spmd.clone, body=%wide.region_2.7_spmd.clone.sunk | while | flops 555874304 | bytes 32605556 | solution.py:92
  244.3 16.0 while.61
  265.4 16.0 while.61
  286.5 16.0 while.61
  307.6 16.0 while.61
  328.7 16.0 while.61
  349.8 16.0 while.61
  370.9 16.0 while.61
  391.9 16.0 while.61
  410.6 13.3 reshape.460
  423.9 10.4 convolution_convert_fusion.1
  443.5 144.7 %reduce-scatter.4.cloned.1.call-done = bf16[2048,1024]{1,0:T(8,128)(2,1)} async-done(((bf16[8192,1024]{1,0:T(8,128)(2,1)}), bf16[2048,1024]{1,0:T(8,128)(2,1)}) %reduce-scatter.4.cloned.1.call-update) | async-done | bytes 4194320 | tf_op jit(solution)/shard_map/reduce_scatter | solution.py:204
  596.3 81.9 %all-gather.7.cloned.1.call-done = bf16[1024,4096]{1,0:T(8,128)(2,1)} async-done(((bf16[1024,1024]{1,0:T(8,128)(2,1)}), bf16[1024,4096]{1,0:T(8,128)(2,1)}) %all-gather.7.cloned.1.call-update) | async-done | bytes 8388624 | tf_op jit(solution)/shard_map/all_gather | solution.py:214
  678.2 98.5 %multiply_convert_fusion.1 = (bf16[2048,4096]{1,0:T(8,128)(2,1)}, f32[2048,4096]{1,0:T(8,128)}, f32[2048,4096]{1,0:T(8,128)}) fusion(f32[4096]{0:T(1024)S(1)} %copy-done.57, bf16[1024,4096]{1,0:T(8,128)(2,1)} %all-gather.7.cloned.1.call-done, f32[1024]{0:T(1024)S(1)} %bitcast.417, f32[1024]{0:T(1024)S(1)} %bitcast.389, f32[2048]{0:T(1024)S(1)} %add_rsqrt_fusion, ...), kind=kOutput, calls=%fused_computation.61 | convolution fusion | flops 17752391680 | bytes 100708352 | tf_op jit(solution)/shard_map/dot_general | solution.py:217
  776.7 40.5 %convert_reduce_fusion = (f32[4096]{0:T(1024)}, bf16[2048,4096]{1,0:T(8,128)(2,1)}) fusion(f32[2048,4096]{1,0:T(8,128)} %get-tuple-element.700, bf16[4096,1024]{1,0:T(8,128)(2,1)} %all-gather.9.cloned.1.call-done, bf16[2048,1024]{1,0:T(8,128)(2,1)} %param.34, f32[2048]{0:T(1024)S(1)} %copy-done.48, f32[2048,4096]{1,0:T(8,128)} %get-tuple-element.753, ...), kind=kOutput, calls=%fused_computation.59 | convolution fusion | flops 17328762880 | bytes 96509952 | tf_op jit(solution)/shard_map/dot_general | solution.py:41
  817.3 29.9 %multiply_reduce_fusion.2 = (f32[1024]{0:T(1024)}, f32[2048]{0:T(1024)S(1)}, f32[2048]{0:T(1024)S(1)}, f32[1024]{0:T(1024)}, f32[2048,1024]{1,0:T(8,128)}) fusion(f32[2048]{0:T(1024)S(1)} %add_rsqrt_fusion, f32[2048]{0:T(1024)S(1)} %broadcast_multiply_fusion.4, f32[1024]{0:T(1024)S(1)} %bitcast.308, ...), kind=kOutput, calls=%fused_computation.107 | convolution fusion | flops 17207128064 | bytes 41992192 | tf_op jit(solution)/shard_map/dot_general | solution.py:41
  847.2 8.5 fusion.94
  861.8 22.7 %convolution_convert_fusion.4 = bf16[4096,1024]{0,1:T(8,128)(2,1)S(1)} fusion(bf16[2048,4096]{1,0:T(8,128)(2,1)} %get-tuple-element.699, bf16[2048,1024]{1,0:T(8,128)(2,1)} %param.34, f32[2048]{0:T(1024)S(1)} %copy-done.48), kind=kOutput, calls=%fused_computation.115 | convolution fusion | flops 17190354944 | bytes 29368320 | tf_op jit(solution)/shard_map/dot_general | solution.py:31
  884.5 26.7 %convolution_convert_fusion.3 = bf16[4096,1024]{0,1:T(8,128)(2,1)} fusion(bf16[2048,4096]{1,0:T(8,128)(2,1)} %get-tuple-element.756, f32[1024]{0:T(1024)S(1)} %bitcast.418, f32[1024]{0:T(1024)S(1)} %bitcast.392, f32[2048]{0:T(1024)S(1)} %add_rsqrt_fusion, f32[2048]{0:T(1024)S(1)} %broadcast_multiply_fusion.4, f32[1024]{0:T(1024)S(1)} %bitcast.310, ...), kind=kOutput, calls=%fused_computation.114 | convolution fusion | flops 17202937856 | bytes 33583104 | tf_op jit(solution)/shard_map/dot_general | solution.py:31
  911.2 10.7 pad_maximum_fusion
  922.4 96.7 %all-gather.11.cloned.1.call-done = bf16[8192,1024]{1,0:T(8,128)(2,1)} async-done(((bf16[2048,1024]{1,0:T(8,128)(2,1)}), bf16[8192,1024]{1,0:T(8,128)(2,1)}) %all-gather.11.cloned.1.call-update) | async-done | bytes 16777232 | tf_op jit(solution)/shard_map/all_gather | solution.py:244
  1019.1 12.4 convolution_convert_fusion.2
  1031.5 13.0 reshape.461
  1044.4 12.9 copy.80
  1057.4 438.8 %while.60 = (s32[]{:T(128)}, bf16[8,1024,4,64]{1,3,2,0:T(8,128)(2,1)}, bf16[8,1024,4,64]{1,3,2,0:T(8,128)(2,1)}, bf16[8,1024,4,64]{1,3,2,0:T(8,128)(2,1)}, f32[8...) while((s32[]{:T(128)}, ...), condition=%wide.region_17.18_spmd.clone, body=%wide.region_13.17_spmd.clone.sunk | while | flops 1368782848 | bytes 155280992 | solution.py:141
  1064.1 44.8 %while.62 = (s32[]{:T(128)}, f32[1024,4,64]{0,2,1:T(8,128)S(1)}, f32[1024,4,64]{0,2,1:T(8,128)S(1)}, bf16[2,512,4,64]{1,3,2,0:T(8,128)(2,1)}, s32[2]{0:T(128)S(1...) while((s32[]{:T(128)}, f32[1024,4,64]{0,2,1:T(8,128)S(1)}, ...), condition=%wide.region_16.16_spmd.clone, body=%wide.region_14.15_spmd.clone.sunk | while | flops 1368782848 | bytes 143712592 | solution.py:138
  1119.8 44.8 %while.62 = (s32[]{:T(128)}, f32[1024,4,64]{0,2,1:T(8,128)S(1)}, f32[1024,4,64]{0,2,1:T(8,128)S(1)}, bf16[2,512,4,64]{1,3,2,0:T(8,128)(2,1)}, s32[2]{0:T(128)S(1...) while((s32[]{:T(128)}, f32[1024,4,64]{0,2,1:T(8,128)S(1)}, ...), condition=%wide.region_16.16_spmd.clone, body=%wide.region_14.15_spmd.clone.sunk | while | flops 1368782848 | bytes 143712592 | solution.py:138
  1175.5 43.7 %while.62 = (s32[]{:T(128)}, f32[1024,4,64]{0,2,1:T(8,128)S(1)}, f32[1024,4,64]{0,2,1:T(8,128)S(1)}, bf16[2,512,4,64]{1,3,2,0:T(8,128)(2,1)}, s32[2]{0:T(128)S(1...) while((s32[]{:T(128)}, f32[1024,4,64]{0,2,1:T(8,128)S(1)}, ...), condition=%wide.region_16.16_spmd.clone, body=%wide.region_14.15_spmd.clone.sunk | while | flops 1368782848 | bytes 143712592 | solution.py:138
  1230.0 43.7 %while.62 = (s32[]{:T(128)}, f32[1024,4,64]{0,2,1:T(8,128)S(1)}, f32[1024,4,64]{0,2,1:T(8,128)S(1)}, bf16[2,512,4,64]{1,3,2,0:T(8,128)(2,1)}, s32[2]{0:T(128)S(1...) while((s32[]{:T(128)}, f32[1024,4,64]{0,2,1:T(8,128)S(1)}, ...), condition=%wide.region_16.16_spmd.clone, body=%wide.region_14.15_spmd.clone.sunk | while | flops 1368782848 | bytes 143712592 | solution.py:138
  1284.6 43.7 %while.62 = (s32[]{:T(128)}, f32[1024,4,64]{0,2,1:T(8,128)S(1)}, f32[1024,4,64]{0,2,1:T(8,128)S(1)}, bf16[2,512,4,64]{1,3,2,0:T(8,128)(2,1)}, s32[2]{0:T(128)S(1...) while((s32[]{:T(128)}, f32[1024,4,64]{0,2,1:T(8,128)S(1)}, ...), condition=%wide.region_16.16_spmd.clone, body=%wide.region_14.15_spmd.clone.sunk | while | flops 1368782848 | bytes 143712592 | solution.py:138
  1339.1 43.7 %while.62 = (s32[]{:T(128)}, f32[1024,4,64]{0,2,1:T(8,128)S(1)}, f32[1024,4,64]{0,2,1:T(8,128)S(1)}, bf16[2,512,4,64]{1,3,2,0:T(8,128)(2,1)}, s32[2]{0:T(128)S(1...) while((s32[]{:T(128)}, f32[1024,4,64]{0,2,1:T(8,128)S(1)}, ...), condition=%wide.region_16.16_spmd.clone, body=%wide.region_14.15_spmd.clone.sunk | while | flops 1368782848 | bytes 143712592 | solution.py:138
  1393.7 43.7 %while.62 = (s32[]{:T(128)}, f32[1024,4,64]{0,2,1:T(8,128)S(1)}, f32[1024,4,64]{0,2,1:T(8,128)S(1)}, bf16[2,512,4,64]{1,3,2,0:T(8,128)(2,1)}, s32[2]{0:T(128)S(1...) while((s32[]{:T(128)}, f32[1024,4,64]{0,2,1:T(8,128)S(1)}, ...), condition=%wide.region_16.16_spmd.clone, body=%wide.region_14.15_spmd.clone.sunk | while | flops 1368782848 | bytes 143712592 | solution.py:138
  1448.2 43.7 %while.62 = (s32[]{:T(128)}, f32[1024,4,64]{0,2,1:T(8,128)S(1)}, f32[1024,4,64]{0,2,1:T(8,128)S(1)}, bf16[2,512,4,64]{1,3,2,0:T(8,128)(2,1)}, s32[2]{0:T(128)S(1...) while((s32[]{:T(128)}, f32[1024,4,64]{0,2,1:T(8,128)S(1)}, ...), condition=%wide.region_16.16_spmd.clone, body=%wide.region_14.15_spmd.clone.sunk | while | flops 1368782848 | bytes 143712592 | solution.py:138
  1496.2 5.9 convert_reduce_fusion.1
  1502.1 22.3 %copy.84 = bf16[8,1024,3,4,64]{1,0,4,3,2:T(8,128)(2,1)S(1)} copy(bf16[8,1024,3,4,64]{1,4,3,0,2:T(8,128)(2,1)S(1)} %get-tuple-element.696) | data formatting | bytes 25165824 | tf_op jit(solution)/shard_map/convert_element_type | solution.py:251
  1524.4 10.7 copy.257
  1535.1 21.1 %convolution_convert_fusion = bf16[8192,1024]{1,0:T(8,128)(2,1)} fusion(bf16[8192,768]{0,1:T(8,128)(2,1)} %bitcast.276, bf16[1024,768]{0,1:T(8,128)(2,1)S(1)} %bitcast.282), kind=kOutput, calls=%fused_computation.79 | convolution fusion | flops 12893290496 | bytes 30932992 | tf_op jit(solution)/shard_map/dot_general | solution.py:41
  1556.3 5.5 copy.87
  1564.2 24.8 %add_convert_fusion.2 = bf16[2048,1024]{1,0:T(8,128)(2,1)} fusion(bf16[2048,4096]{1,0:T(8,128)(2,1)} %get-tuple-element.699, bf16[4096,1024]{1,0:T(8,128)(2,1)} %all-gather.9.cloned.1.call-done, f32[1024]{0:T(1024)S(1)} %bitcast.416, f32[1024]{0:T(1024)S(1)} %bitcast.311, bf16[2048,1024]{1,0:T(8,128)(2,1)} %reduce-scatter.4.cloned.1.call-done, ...), kind=kOutput, calls=%fused_computation.110 | convolution fusion | flops 17194549248 | bytes 37756928 | tf_op jit(solution)/shard_map/dot_general | solution.py:219
  1589.2 10.0 convolution_add_fusion
  1601.2 19.7 bitcast_add_fusion
  1633.6 25.7 %all-reduce.2 = (bf16[1024,8]{0,1:T(8,128)(2,1)S(1)}, bf16[256,8]{0,1:T(8,128)(2,1)S(1)}, bf16[1024,8]{0,1:T(8,128)(2,1)S(1)}, bf16[1024,8]{0,1:T(8,128)(2,1)S(1)}) all-reduce(bf16[1024,8]{0,1:T(8,128)(2,1)S(1)} %convolution_convert_fusion.10, ...), channel_id=1, replica_groups=mesh['dp'=8,'tensor'=4] {'dp'}, use_global_device_ids=true, to_apply=%region_32.33 | all-reduce | flops 26624 | bytes 106496 | tf_op jit(solution)/shard_map/psum | solution.py:303
  1672.8 6.4 multiply_reduce_fusion.11
  1715.5 6.2 multiply_reduce_fusion.47
  1758.1 6.2 multiply_reduce_fusion.119
  1800.2 6.5 multiply_reduce_fusion.83
  1829.8 17.7 subtract_multiply_fusion.1
  1847.5 17.6 subtract_multiply_fusion.8
  1865.2 17.4 subtract_multiply_fusion.22
  1882.7 18.0 subtract_multiply_fusion.15
  1905.4 7.2 convolution_convert_fusion.5
  1915.0 26.6 %all-reduce.1 = (bf16[768,8]{0,1:T(8,128)(2,1)S(1)}, bf16[1024,8]{0,1:T(8,128)(2,1)S(1)}, bf16[1024,8]{0,1:T(8,128)(2,1)S(1)}, bf16[1024,8]{0,1:T(8,128)(2,1)S(1)}) all-reduce(bf16[768,8]{0,1:T(8,128)(2,1)S(1)} %convolution_convert_fusion.11, ...), channel_id=1, replica_groups=mesh['dp'=8,'tensor'=4] {'dp'}, use_global_device_ids=true, to_apply=%region_69.70 | all-reduce | flops 30720 | bytes 122880 | tf_op jit(solution)/shard_map/psum | solution.py:311
  1941.7 9.1 multiply_subtract_fusion
  1956.1 8.6 subtract_bitcast_fusion
  1964.7 5.3 copy.90
  1987.2 7.1 multiply_subtract_fusion.2
  1996.0 8.8 multiply_subtract_fusion.1
  2004.9 6.3 fusion.61
  2011.4 43.7 %all-reduce = (f32[6,1024]{1,0:T(8,128)S(1)}, f32[2,1024]{1,0:T(2,128)S(1)}, f32[4096]{0:T(1024)S(1)}) all-reduce(f32[6,1024]{1,0:T(8,128)S(1)} %stack.42, f32[2,1024]{1,0:T(2,128)S(1)} %maximum_dynamic-update-slice_fusion, f32[4096]{0:T(1024)S(1)} %copy-done.60), channel_id=1, replica_groups=mesh['dp'=8,'tensor'=4] {'dp','tensor'}, use_global_device_ids=true, to_apply=%region_27.28 | all-reduce | flops 12288 | bytes 98304 | tf_op jit(solution)/shard_map/psum | solution.py:282
  2057.0 9.5 fusion.57
  (811 shorter events, 768.8 us)
Async XLA Ops:
  7.2 1618.9 %copy-start = (f32[1,1024,8]{1,2,0:T(8,128)S(1)}, f32[1,1024,8]{1,2,0:T(8,128)}, u32[]{:S(2)}) copy-start(f32[1,1024,8]{1,2,0:T(8,128)} %param.57) | copy-start | bytes 98308
  7.2 169.8 %all-gather.5.cloned.1.call-start = ((), (), s32[]{:S(2)}) async-start(), calls=%async_computation.3 | async-start | bytes 20971520 | tf_op jit(solution)/shard_map/all_gather | solution.py:188
  7.3 8.2 copy-start.4
  18.5 569.8 %reduce-scatter.4.cloned.1.call-start = ((), (), s32[]{:S(2)}) async-start(), calls=%async_computation.4 | async-start | bytes 20971520 | tf_op jit(solution)/shard_map/reduce_scatter | solution.py:204
  410.6 13.3 copy-start.25
  434.4 153.9 %copy-start.43 = (f32[1,1024]{1,0:T(1,128)S(1)}, f32[1,1024]{1,0:T(1,128)}, u32[]{:S(2)}) copy-start(f32[1,1024]{1,0:T(1,128)} %get-tuple-element.718) | copy-start | bytes 12292
  434.4 243.8 %all-gather.7.cloned.1.call-start = ((), (), s32[]{:S(2)}) async-start(), calls=%async_computation.5 | async-start | bytes 10485760 | tf_op jit(solution)/shard_map/all_gather | solution.py:214
  438.3 338.4 %all-gather.9.cloned.1.call-start = ((), (), s32[]{:S(2)}) async-start(), calls=%async_computation.6 | async-start | bytes 10485760 | tf_op jit(solution)/shard_map/all_gather | solution.py:215
  442.2 576.9 %all-gather.11.cloned.1.call-start = ((), (), s32[]{:S(2)}) async-start(), calls=%async_computation.7 | async-start | bytes 20971520 | tf_op jit(solution)/shard_map/all_gather | solution.py:244
  588.3 89.9 %copy-start.56 = (f32[1,1024]{1,0:T(1,128)S(1)}, f32[1,1024]{1,0:T(1,128)}, u32[]{:S(2)}) copy-start(f32[1,1024]{1,0:T(1,128)} %get-tuple-element.717) | copy-start | bytes 12292
  588.3 89.9 %copy-start.57 = (f32[4096]{0:T(1024)S(1)}, f32[4096]{0:T(1024)}, u32[]{:S(2)}) copy-start(f32[4096]{0:T(1024)} %param.38) | copy-start | bytes 49156
  588.3 89.9 %copy-start.65 = (f32[1,1024]{1,0:T(1,128)S(1)}, f32[1,1024]{1,0:T(1,128)}, u32[]{:S(2)}) copy-start(f32[1,1024]{1,0:T(1,128)} %get-tuple-element.716) | copy-start | bytes 12292
  678.2 98.5 %copy-start.48 = (f32[2048]{0:T(1024)S(1)}, f32[2048]{0:T(1024)}, u32[]{:S(2)}) copy-start(f32[2048]{0:T(1024)} %fusion.85) | copy-start | bytes 24580
  817.3 29.9 %copy-start.6 = (bf16[2048,1024]{1,0:T(8,128)(2,1)S(1)}, bf16[2048,1024]{1,0:T(8,128)(2,1)}, u32[]{:S(2)}) copy-start(bf16[2048,1024]{1,0:T(8,128)(2,1)} %param.33) | copy-start | bytes 12582916
  817.3 29.9 %copy-start.16 = (bf16[2048,1024]{1,0:T(8,128)(2,1)S(1)}, bf16[2048,1024]{1,0:T(8,128)(2,1)}, u32[]{:S(2)}) copy-start(bf16[2048,1024]{1,0:T(8,128)(2,1)} %reduce-scatter.4.cloned.1.call-done) | copy-start | bytes 12582916
  817.3 29.9 %copy-start.28 = (bf16[2048,1024]{1,0:T(8,128)(2,1)S(1)}, bf16[2048,1024]{1,0:T(8,128)(2,1)}, u32[]{:S(2)}) copy-start(bf16[2048,1024]{1,0:T(8,128)(2,1)} %param.34) | copy-start | bytes 12582916
  861.7 760.9 %reduce-scatter.8.cloned.1.call-start = ((), (), s32[]{:S(2)}) async-start(), calls=%async_computation.9 | async-start | bytes 20971520 | tf_op jit(solution)/shard_map/reduce_scatter | solution.py:226
  861.7 22.7 %copy-start.7 = (bf16[2048,1024]{1,0:T(8,128)(2,1)S(1)}, bf16[2048,1024]{1,0:T(8,128)(2,1)}, u32[]{:S(2)}) copy-start(bf16[2048,1024]{1,0:T(8,128)(2,1)} %param.33) | copy-start | bytes 12582916
  861.8 22.7 %copy-start.17 = (bf16[2048,1024]{1,0:T(8,128)(2,1)S(1)}, bf16[2048,1024]{1,0:T(8,128)(2,1)}, u32[]{:S(2)}) copy-start(bf16[2048,1024]{1,0:T(8,128)(2,1)} %reduce-scatter.4.cloned.1.call-done) | copy-start | bytes 12582916
  922.0 97.2 %copy-start.26 = (f32[256,1024]{1,0:T(8,128)S(1)}, f32[256,1024]{1,0:T(8,128)}, u32[]{:S(2)}) copy-start(f32[256,1024]{1,0:T(8,128)} %param.40) | copy-start | bytes 3145732
  922.0 1082.9 %reduce-scatter.6.cloned.1.call-start = ((), (), s32[]{:S(2)}) async-start(), calls=%async_computation.8 | async-start | bytes 20971520 | tf_op jit(solution)/shard_map/reduce_scatter | solution.py:262
  1075.8 8.8 copy-start.2
  1098.2 8.8 copy-start.2
  1131.5 8.8 copy-start.2
  1153.9 8.8 copy-start.2
  1187.1 8.3 copy-start.2
  1209.0 8.3 copy-start.2
  1241.7 8.3 copy-start.2
  1263.6 8.3 copy-start.2
  1296.3 8.3 copy-start.2
  1318.1 8.3 copy-start.2
  1350.8 8.3 copy-start.2
  1372.7 8.3 copy-start.2
  1405.4 8.3 copy-start.2
  1427.2 8.3 copy-start.2
  1459.9 8.3 copy-start.2
  1481.8 8.3 copy-start.2
  1524.4 10.7 copy-start.31
  1556.2 7.9 copy-start.44
  1556.2 7.9 copy-start.64
  1564.1 25.0 %copy-start.32 = (f32[1,256,1024]{2,1,0:T(8,128)S(1)}, f32[1,256,1024]{2,1,0:T(8,128)}, u32[]{:S(2)}) copy-start(f32[1,256,1024]{2,1,0:T(8,128)} %param.51) | copy-start | bytes 3145732
  1589.2 11.0 copy-start.49
  1589.2 11.9 copy-start.30
  1601.1 19.7 copy-start.53
  1847.5 94.2 %copy-start.34 = (f32[1024,8]{0,1:T(8,128)}, f32[1024,8]{0,1:T(8,128)S(1)}, u32[]{:S(2)}) copy-start(f32[1024,8]{0,1:T(8,128)S(1)} %stack.47) | copy-start | bytes 98308
  1865.2 129.1 %copy-start.36 = (f32[1024,8]{0,1:T(8,128)}, f32[1024,8]{0,1:T(8,128)S(1)}, u32[]{:S(2)}) copy-start(f32[1024,8]{0,1:T(8,128)S(1)} %stack.46) | copy-start | bytes 98308
  1882.7 101.7 %copy-start.42 = (f32[256,8]{0,1:T(8,128)}, f32[256,8]{0,1:T(8,128)S(1)}, u32[]{:S(2)}) copy-start(f32[256,8]{0,1:T(8,128)S(1)} %stack.45) | copy-start | bytes 24580
  1900.7 69.4 %copy-start.35 = (f32[1024,8]{0,1:T(8,128)}, f32[1024,8]{0,1:T(8,128)S(1)}, u32[]{:S(2)}) copy-start(f32[1024,8]{0,1:T(8,128)S(1)} %stack.44) | copy-start | bytes 98308
  1900.7 11.9 copy-start.9
  1900.7 11.9 copy-start.13
  1974.6 9.7 copy-start.19
  1974.6 9.7 copy-start.27
  1974.6 9.7 copy-start.33
  1984.3 10.0 slice-start
  1987.2 8.8 copy-start.20
  1996.0 8.9 copy-start.38
  1996.0 8.9 copy-start.40
  1996.0 8.9 copy-start.46
  2004.8 50.3 %copy-start.41 = (f32[6,1024]{1,0:T(8,128)S(1)}, f32[6,1024]{1,0:T(8,128)}, u32[]{:S(2)}) copy-start(f32[6,1024]{1,0:T(8,128)} %param.36) | copy-start | bytes 73732
  2004.8 50.3 %copy-start.50 = (f32[6,1024]{1,0:T(8,128)S(1)}, f32[6,1024]{1,0:T(8,128)}, u32[]{:S(2)}) copy-start(f32[6,1024]{1,0:T(8,128)} %param.43) | copy-start | bytes 73732
  2004.8 50.9 %copy-start.58 = (f32[4096]{0:T(1024)S(1)}, f32[4096]{0:T(1024)}, u32[]{:S(2)}) copy-start(f32[4096]{0:T(1024)} %param.38) | copy-start | bytes 49156
  2004.8 50.9 %copy-start.59 = (f32[4096]{0:T(1024)S(1)}, f32[4096]{0:T(1024)}, u32[]{:S(2)}) copy-start(f32[4096]{0:T(1024)} %param.45) | copy-start | bytes 49156
  2004.9 51.5 %copy-start.52 = (f32[2,1024]{1,0:T(2,128)S(1)}, f32[2,1024]{1,0:T(2,128)}, u32[]{:S(2)}) copy-start(f32[2,1024]{1,0:T(2,128)} %param.37) | copy-start | bytes 24580
  2004.9 51.5 %copy-start.61 = (f32[2,1024]{1,0:T(2,128)S(1)}, f32[2,1024]{1,0:T(2,128)}, u32[]{:S(2)}) copy-start(f32[2,1024]{1,0:T(2,128)} %param.44) | copy-start | bytes 24580
  (86 other events, 278.5 us)
Sparse Core Ops, SparseCore 0:
  18.6 158.4 all-gather.4
  434.5 153.7 reduce-scatter.3
  590.7 87.4 all-gather.6
  680.5 87.4 all-gather.8
  861.8 157.2 all-gather.10
  1022.0 153.7 reduce-scatter.7
  1556.3 153.7 reduce-scatter.5
where the time goes:
time: 2080 us; the launch traced here: 2070 us
  matrix products  687 us (33%)
  waiting for transfers between devices  480 us (23%)
  other arithmetic  392 us (19%)
  local copies, waits for them, and re-layouts  315 us (15%)
  blocking collectives  96 us (5%)
  loops' own time  64.9 us (3%)
  between operations  38.1 us (2%)
    all_gather x1, waiting for transfers between devices, shards(): gathered_one = lax.all_gather(ln_one, 'tensor', axis=0, tiled=True)  156 us
    reduce_scatter x1, waiting for transfers between devices, shards(): lax.psum_scatter(jnp.dot(context_rows, out_weight, preferred_element_type...  145 us
    dot_general x8, matrix products, times_trans(): lax.dot_general(left_mat, right_mat, (((1,), (1,)), ((), ())), precision=...  129 us
    reduce_sum x37, other arithmetic, orthonormal(): vector = vector - jnp.sum(column * vector, axis=-1, keepdims=True) * column  113 us
    dot_general x1, matrix products, shards(): jnp.dot(ln_two, up_full, preferred_element_type=jnp.float32) + up_bias  98.5 us
    all_gather x1, waiting for transfers between devices, shards(): grad_attn_all = lax.all_gather(grad_attn, 'tensor', axis=0, tiled=True)  96.7 us
    dot_general x8, matrix products, inner_rows(): lax.dot_general(left_mat, right_mat, (((0,), (0,)), ((), ())), precision=...  93.4 us
    all_gather x1, waiting for transfers between devices, shards(): lax.all_gather(w_up.astype(jnp.bfloat16), 'tensor', axis=1, tiled=True)  81.9 us
  transfers between devices with their start and end apart: 7, of which 4 were waited for; matrix products, arithmetic and copies ran while one was open for 50% of the time, Pallas kernels for 0%

commit v1 on v0

v1 whole, which is shorter than its diff:
```python
import functools

import jax
import jax.numpy as jnp
from jax import lax
from jax.experimental import pallas as pl
from jax.experimental.pallas import tpu as pltpu
from jax.sharding import PartitionSpec as P

HEAD_DIM = 64
CLIP_LEN = 1024
LANES = 128

PRECISE = lax.Precision.HIGHEST
NORM_EPS = 1e-06
STEP_RATE = 0.001
VECTOR_RATE = 0.015
MOMENTUM_DECAY = 0.9


def layer_norm(values):
    centre = values - jnp.mean(values, axis=-1, keepdims=True)
    spread = jnp.mean(centre * centre, axis=-1, keepdims=True)
    inv_std = lax.rsqrt(spread + NORM_EPS)
    return (centre * inv_std, inv_std)


def norm_back(grad_norm, normed, inv_std):
    mean_grad = jnp.mean(grad_norm, axis=-1, keepdims=True)
    mean_cross = jnp.mean(grad_norm * normed, axis=-1, keepdims=True)
    return inv_std * (grad_norm - mean_grad - normed * mean_cross)


def dot_on(left_dim, right_dim, left_mat, right_mat, precision=None):
    return lax.dot_general(
        left_mat,
        right_mat,
        (((left_dim,), (right_dim,)), ((), ())),
        precision=precision,
        preferred_element_type=jnp.float32,
    )


inner_rows = functools.partial(dot_on, 0, 0)
times_trans = functools.partial(dot_on, 1, 1)
times = functools.partial(dot_on, 1, 0)


def gelu_parts(pre_act):
    size = jnp.abs(pre_act) * (0.5**0.5)
    bell = jnp.exp(-size * size)
    inv = 1.0 / (1.0 + 0.3275911 * size)
    series = 1.061405429 * inv - 1.453152027
    series = series * inv + 1.421413741
    series = series * inv - 0.284496736
    series = series * inv + 0.254829592
    tail = 0.5 * series * inv * bell
    cdf = jnp.where(pre_act >= 0, 1.0 - tail, tail)
    return (pre_act * cdf, cdf + pre_act * bell * 0.3989422804014327)


def head_masks(rows):
    lane = lax.broadcasted_iota(jnp.int32, (rows, LANES), 1)
    return [lane // HEAD_DIM == pos for pos in range(LANES // HEAD_DIM)]


def only(mask, values):
    return jnp.where(mask, values, jnp.zeros_like(values))


def forward_body(scale, tile, q_ref, k_ref, v_ref, ctx_ref, lse_ref, k_heads, v_heads):
    masks = head_masks(k_ref.shape[0])
    for pos, mask in enumerate(masks):
        k_heads[pos] = only(mask, k_ref[...])
        v_heads[pos, :, :LANES] = only(mask, v_ref[...])
        v_heads[pos, :, LANES:] = mask.astype(jnp.bfloat16)
    tile_masks = head_masks(tile)

    def step(pos, carry):
        rows = pl.ds(pl.multiple_of(pos * tile, tile), tile)
        q_tile = q_ref[rows, :] * scale
        total = jnp.zeros((tile, 2 * LANES), jnp.float32)
        tops = []
        for head in range(len(masks)):
            scores = times_trans(q_tile, k_heads[head])
            top = jnp.max(scores, axis=1, keepdims=True)
            weights = jnp.exp(scores - top).astype(jnp.bfloat16)
            total = total + times(weights, v_heads[head])
            tops.append(top)
        sums = total[:, LANES:]
        ctx_ref[rows, :] = (total[:, :LANES] / sums).astype(jnp.bfloat16)
        lse_ref[rows, :] = jnp.where(tile_masks[0], tops[0], tops[1]) + jnp.log(sums)
        return carry

    lax.fori_loop(0, q_ref.shape[0] // tile, step, 0, unroll=True)


def backward_body(
    scale, tile, q_ref, k_ref, v_ref, ctx_ref, lse_ref, do_ref, dq_ref, dk_ref, dv_ref, k_heads, v_heads, dk_sum, dv_sum
):
    masks = head_masks(k_ref.shape[0])
    for pos, mask in enumerate(masks):
        k_heads[pos] = only(mask, k_ref[...])
        v_heads[pos] = only(mask, v_ref[...])
    tile_masks = head_masks(tile)
    dk_sum[...] = jnp.zeros_like(dk_sum)
    dv_sum[...] = jnp.zeros_like(dv_sum)

    def step(pos, carry):
        rows = pl.ds(pl.multiple_of(pos * tile, tile), tile)
        q_tile = q_ref[rows, :] * scale
        do_tile = do_ref[rows, :]
        lse = lse_ref[rows, :]
        cross = do_tile.astype(jnp.float32) * ctx_ref[rows, :].astype(jnp.float32)
        grad_q = jnp.zeros((tile, LANES), jnp.float32)
        for head, mask in enumerate(tile_masks):
            scores = times_trans(q_tile, k_heads[head])
            lane = head * HEAD_DIM
            probs = jnp.exp(scores - lse[:, lane : lane + 1])
            inner = jnp.sum(only(mask, cross), axis=1, keepdims=True)
            grad_p = times_trans(do_tile, v_heads[head])
            grad_s = (probs * (grad_p - inner)).astype(jnp.bfloat16)
            grad_q = grad_q + times(grad_s, k_heads[head])
            dk_sum[...] += inner_rows(grad_s, only(mask, q_tile))
            dv_sum[...] += inner_rows(probs.astype(jnp.bfloat16), only(mask, do_tile))
        dq_ref[rows, :] = (grad_q * scale).astype(jnp.bfloat16)
        return carry

    lax.fori_loop(0, q_ref.shape[0] // tile, step, 0, unroll=True)
    dk_ref[...] = dk_sum[...].astype(jnp.bfloat16)
    dv_ref[...] = dv_sum[...].astype(jnp.bfloat16)


def joined_forward(scale, tile, qkv_ref, *refs):
    parts = [qkv_ref.at[:, pos * LANES : (pos + 1) * LANES] for pos in range(3)]
    forward_body(scale, tile, *parts, *refs)


def joined_backward(scale, tile, qkv_ref, ctx_ref, lse_ref, do_ref, grad_ref, *scratch):
    parts = [qkv_ref.at[:, pos * LANES : (pos + 1) * LANES] for pos in range(3)]
    grads = [grad_ref.at[:, pos * LANES : (pos + 1) * LANES] for pos in range(3)]
    backward_body(scale, tile, *parts, ctx_ref, lse_ref, do_ref, *grads, *scratch)


def block_of(rows, width):
    return pl.BlockSpec((rows, width), lambda clip, block: (clip, block))


def attention_forward(arrays, clips, tile=256):
    joined = len(arrays) == 1
    q_rows, k_rows = arrays[0].shape[0] // clips, arrays[-1].shape[0] // clips
    blocks = arrays[0].shape[1] // (LANES * (3 if joined else 1))
    work = clips * blocks * 2 * q_rows * k_rows
    in_specs = [block_of(q_rows, 3 * LANES)] if joined else [block_of(q_rows, LANES), block_of(k_rows, LANES), block_of(k_rows, LANES)]
    return pl.pallas_call(
        functools.partial(joined_forward if joined else forward_body, HEAD_DIM**-0.5, min(tile, q_rows)),
        grid=(clips, blocks),
        in_specs=in_specs,
        out_specs=[block_of(q_rows, LANES), block_of(q_rows, LANES)],
        out_shape=[
            jax.ShapeDtypeStruct((clips * q_rows, blocks * LANES), dtype)
            for dtype in (jnp.bfloat16, jnp.float32)
        ],
        scratch_shapes=[
            pltpu.VMEM((2, k_rows, LANES), jnp.bfloat16),
            pltpu.VMEM((2, k_rows, 2 * LANES), jnp.bfloat16),
        ],
        cost_estimate=pl.CostEstimate(
            flops=1024 * work, transcendentals=work, bytes_accessed=12 * clips * blocks * q_rows * LANES
        ),
        name="attn_fwd",
    )(*arrays)


def attention_backward(arrays, ctx, lse, grad_ctx, clips, tile=256):
    joined = len(arrays) == 1
    q_rows, k_rows = arrays[0].shape[0] // clips, arrays[-1].shape[0] // clips
    blocks = ctx.shape[1] // LANES
    work = clips * blocks * 2 * q_rows * k_rows
    shared = [block_of(q_rows, LANES) for _ in range(3)]
    if joined:
        in_specs = [block_of(q_rows, 3 * LANES)] + shared
        out_specs = [block_of(q_rows, 3 * LANES)]
        out_shape = [jax.ShapeDtypeStruct(arrays[0].shape, jnp.bfloat16)]
    else:
        in_specs = [block_of(q_rows, LANES), block_of(k_rows, LANES), block_of(k_rows, LANES)] + shared
        out_specs = [block_of(q_rows, LANES), block_of(k_rows, LANES), block_of(k_rows, LANES)]
        out_shape = [jax.ShapeDtypeStruct(array.shape, jnp.bfloat16) for array in arrays]
    return pl.pallas_call(
        functools.partial(joined_backward if joined else backward_body, HEAD_DIM**-0.5, min(tile, q_rows)),
        grid=(clips, blocks),
        in_specs=in_specs,
        out_specs=out_specs,
        out_shape=out_shape,
        scratch_shapes=[
            pltpu.VMEM((2, k_rows, LANES), jnp.bfloat16),
            pltpu.VMEM((2, k_rows, LANES), jnp.bfloat16),
            pltpu.VMEM((k_rows, LANES), jnp.float32),
            pltpu.VMEM((k_rows, LANES), jnp.float32),
        ],
        cost_estimate=pl.CostEstimate(
            flops=2560 * work, transcendentals=work, bytes_accessed=20 * clips * blocks * q_rows * LANES
        ),
        name="attn_bwd",
    )(*arrays, ctx, lse, grad_ctx)


def orthonormal_body(count, *refs):
    values = [ref[...] for ref in refs[:count]]
    rank = values[0].shape[0]
    rows = [lax.broadcasted_iota(jnp.int32, (rank, 1), 0) for _ in values]
    for pos in range(rank):
        for which, value in enumerate(values):
            vector = value[pos : pos + 1, :]
            vector = vector * lax.rsqrt(jnp.sum(vector * vector, axis=1, keepdims=True) + 1e-12)
            along = jnp.sum(value * vector, axis=1, keepdims=True)
            later = jnp.where(rows[which] > pos, value - along * vector, value)
            values[which] = jnp.where(rows[which] == pos, vector, later)
    for ref, value in zip(refs[count:], values):
        ref[...] = value


def orthonormal(lefts):
    return pl.pallas_call(
        functools.partial(orthonormal_body, len(lefts)),
        out_shape=[jax.ShapeDtypeStruct(left.shape, jnp.float32) for left in lefts],
        name="orthonormal",
    )(*lefts)


def psum_joined(parts, axis):
    joined = lax.psum(jnp.concatenate(parts, axis=1).astype(jnp.bfloat16), axis).astype(jnp.float32)
    ends = [0]
    for part in parts:
        ends.append(ends[-1] + part.shape[1])
    return [joined[:, start:end] for start, end in zip(ends, ends[1:])]


def shards(
    tokens,
    cotangent,
    clip_counts,
    norm_params,
    head_bias,
    up_bias,
    w_qkv,
    w_out,
    w_up,
    w_down,
    mom_norm,
    mom_head_bias,
    mom_up_bias,
    mom_qkv,
    mom_out,
    mom_up,
    mom_down,
    err_qkv,
    err_out,
    err_up,
    err_down,
    basis_qkv,
    basis_out,
    basis_up,
    basis_down,
):
    tensor_count = lax.axis_size("tensor")
    tensor_pos = lax.axis_index("tensor")
    replica_count = lax.axis_size("dp")
    local_rows, model_width = tokens.shape
    width_loc = w_out.shape[0]
    hidden_loc = w_up.shape[1]
    clips = max(1, local_rows // CLIP_LEN)
    sharers = max(1, CLIP_LEN // local_rows)
    halves = 2 if width_loc % (2 * LANES) == 0 and replica_count % 2 == 0 and sharers == 1 else 1
    width_half, hidden_half = width_loc // halves, hidden_loc // halves
    core = lax.axis_index("dp") % halves
    part_ids = [core, 1 - core][:halves]

    def half_of(whole, axis):
        if halves == 1:
            return whole
        size = whole.shape[axis] // halves
        return lax.dynamic_slice_in_dim(whole, core * size, size, axis)

    def all_halves(half, axis):
        gathered = lax.all_gather(half, "tensor", axis=axis, tiled=True)
        if halves == 1:
            return [gathered]
        swap = [(pos, pos ^ 1) for pos in range(replica_count)]
        return [gathered, lax.ppermute(gathered, "dp", swap)]

    def in_order(parts, axis):
        if halves == 1:
            return parts[0]
        return jnp.where(core == 0, jnp.concatenate(parts, axis), jnp.concatenate(parts[::-1], axis))

    def vector_part(vector, part_id, width):
        return lax.dynamic_index_in_dim(vector.reshape(tensor_count, halves, width), part_id, 1, False)

    low = jnp.bfloat16
    row_ids = tensor_pos * local_rows + jnp.arange(local_rows, dtype=jnp.int32)
    live_rows = (row_ids // CLIP_LEN < clip_counts[0]).astype(jnp.float32)
    grad_rows = (cotangent.astype(jnp.float32) * live_rows[:, None]).astype(low)

    qkv_half = half_of(w_qkv.astype(low).reshape(model_width, 3, width_loc), 2)
    qkv_ws = all_halves(qkv_half.reshape(model_width, 3 * width_half), 1)
    out_ws = all_halves(half_of(w_out.astype(low), 0), 0)
    up_ws = all_halves(half_of(w_up.astype(low), 1), 1)
    down_ws = all_halves(half_of(w_down.astype(low), 0), 0)

    inputs_f = tokens.astype(jnp.float32)
    normed_one, inv_one = layer_norm(inputs_f)
    ln_one = (normed_one * norm_params[0] + norm_params[1]).astype(low)

    def split_heads(rows_qkv):
        parts = jnp.moveaxis(rows_qkv.reshape(local_rows, tensor_count, 3, width_half), 2, 0)
        parts = parts.reshape(3, local_rows, tensor_count * width_half)
        return [parts[0]] + [share(part) for part in parts[1:]]

    def share(part):
        others = [
            lax.ppermute(part, "tensor", [(pos, pos ^ step) for pos in range(tensor_count)])
            for step in range(1, sharers)
        ]
        return jnp.concatenate([part] + others, axis=0)

    def unshare(grad):
        pieces = grad.reshape(sharers, local_rows, grad.shape[1])
        total = pieces[0].astype(jnp.float32)
        for step in range(1, sharers):
            back = lax.ppermute(pieces[step], "tensor", [(pos, pos ^ step) for pos in range(tensor_count)])
            total = total + back.astype(jnp.float32)
        return total.astype(low)

    joined = width_half % LANES == 0 and width_half == LANES and sharers == 1
    qkvs, contexts, log_sums = [], [], []
    for qkv_w, part_id in zip(qkv_ws, part_ids):
        bias_q = vector_part(head_bias[0], part_id, width_half)
        bias_v = vector_part(head_bias[1], part_id, width_half)
        bias = jnp.stack([bias_q, jnp.zeros_like(bias_q), bias_v], axis=1).reshape(-1)
        rows_qkv = (times(ln_one, qkv_w) + bias).astype(low)
        arrays = [rows_qkv] if joined else split_heads(rows_qkv)
        context, log_sum = attention_forward(arrays, clips)
        qkvs.append(arrays)
        contexts.append(context)
        log_sums.append(log_sum)
    attn_sum = sum(times(context, out_w) for context, out_w in zip(contexts, out_ws))
    resid_one = inputs_f + attn_sum + norm_params[2]
    normed_two, inv_two = layer_norm(resid_one)
    ln_two = (normed_two * norm_params[3] + norm_params[4]).astype(low)

    hiddens, slopes = [], []
    for up_w, part_id in zip(up_ws, part_ids):
        bias = vector_part(up_bias, part_id, hidden_half).reshape(-1)
        hidden, slope = gelu_parts(times(ln_two, up_w) + bias)
        hidden, slope = lax.optimization_barrier((hidden.astype(low), slope.astype(low)))
        hiddens.append(hidden)
        slopes.append(slope)
    ffn_sum = sum(times(hidden, down_w) for hidden, down_w in zip(hiddens, down_ws))
    block_out = (resid_one + ffn_sum + norm_params[5]).astype(low)

    def scatter(grad, axis):
        return lax.psum_scatter(grad.astype(low), "tensor", scatter_dimension=axis, tiled=True).astype(jnp.float32)

    grads_pre, up_bias_parts, down_parts, up_parts = [], [], [], []
    for hidden, slope, down_w in zip(hiddens, slopes, down_ws):
        grad_pre = (times_trans(grad_rows, down_w) * slope.astype(jnp.float32)).astype(low)
        grads_pre.append(grad_pre)
        up_bias_parts.append(jnp.sum(grad_pre.astype(jnp.float32), axis=0).reshape(tensor_count, hidden_half))
        down_parts.append(scatter(inner_rows(hidden, grad_rows), 0))
        up_parts.append(scatter(inner_rows(ln_two, grad_pre), 1))
    grad_ln_two = sum(times_trans(grad_pre, up_w) for grad_pre, up_w in zip(grads_pre, up_ws))
    grad_down = in_order(down_parts, 0)
    grad_up = in_order(up_parts, 1)
    grad_res_one = grad_rows.astype(jnp.float32) + norm_back(
        grad_ln_two * norm_params[3], normed_two, inv_two
    )
    gain_two_grad = jnp.sum(grad_ln_two * normed_two, axis=0)
    shift_two_grad = jnp.sum(grad_ln_two, axis=0)
    down_bias_grad = jnp.sum(grad_rows.astype(jnp.float32), axis=0)
    out_bias_grad = jnp.sum(grad_res_one, axis=0)
    grad_attn = grad_res_one.astype(low)

    out_parts, qkv_parts, bias_parts, grads_in = [], [], [], []
    for context, log_sum, arrays, out_w, qkv_w in zip(contexts, log_sums, qkvs, out_ws, qkv_ws):
        out_parts.append(scatter(inner_rows(context, grad_attn), 0))
        grad_context = times_trans(grad_attn, out_w).astype(low)
        grads = attention_backward(arrays, context, log_sum, grad_context, clips)
        if joined:
            grad_qkv = grads[0]
        else:
            grads = [grads[0]] + [unshare(grad) for grad in grads[1:]]
            grads = [grad.reshape(local_rows, tensor_count, 1, width_half) for grad in grads]
            grad_qkv = jnp.concatenate(grads, axis=2).reshape(local_rows, -1)
        qkv_parts.append(scatter(inner_rows(ln_one, grad_qkv), 1))
        bias_parts.append(jnp.sum(grad_qkv.astype(jnp.float32), axis=0).reshape(tensor_count, 3, width_half))
        grads_in.append(times_trans(grad_qkv, qkv_w))
    grad_out_w = in_order(out_parts, 0)
    grad_qkv_w = in_order([part.reshape(model_width, 3, width_half) for part in qkv_parts], 2)
    grad_qkv_w = grad_qkv_w.reshape(model_width, 3 * width_loc)
    grad_ln_one = sum(grads_in)

    def whole_vector(parts):
        parts = [part[:, None, :] for part in parts]
        return in_order(parts, 1).reshape(-1)

    grad_head_bias = jnp.stack([whole_vector([part[:, pos] for part in bias_parts]) for pos in (0, 2)])
    grad_up_bias = whole_vector(up_bias_parts)
    grad_input = grad_res_one + norm_back(grad_ln_one * norm_params[0], normed_one, inv_one)
    input_grad = grad_input.astype(low)
    gain_one_grad = jnp.sum(grad_ln_one * normed_one, axis=0)
    shift_one_grad = jnp.sum(grad_ln_one, axis=0)
    grad_norm = jnp.stack(
        [
            gain_one_grad,
            shift_one_grad,
            out_bias_grad,
            gain_two_grad,
            shift_two_grad,
            down_bias_grad,
        ]
    )
    sum_norm, sum_head, sum_up = lax.psum(
        (grad_norm, grad_head_bias, grad_up_bias), ("dp", "tensor")
    )
    new_vecs = []
    new_vec_moms = []
    for param_now, moment_now, grad_sum in zip(
        (norm_params, head_bias, up_bias),
        (mom_norm, mom_head_bias, mom_up_bias),
        (sum_norm, sum_head, sum_up),
    ):
        moment_new = MOMENTUM_DECAY * moment_now + grad_sum / replica_count
        new_vec_moms.append(moment_new)
        new_vecs.append(param_now - VECTOR_RATE * moment_new)
    grads_local = (grad_qkv_w, grad_out_w, grad_up, grad_down)
    errors_local = (err_qkv.reshape(model_width, 3 * width_loc), err_out[0], err_up[0], err_down[0])
    factors_local = (basis_qkv[0], basis_out[0], basis_up[0], basis_down[0])
    merged = [grad_now + error_now for grad_now, error_now in zip(grads_local, errors_local)]
    lefts = [
        dot_on(0, 1, factor, matrix, PRECISE) for matrix, factor in zip(merged, factors_local)
    ]
    orthos = orthonormal(psum_joined(lefts, "dp"))
    rights = [times(ortho_left, matrix, PRECISE) for matrix, ortho_left in zip(merged, orthos)]
    right_means = [right_sum / replica_count for right_sum in psum_joined(rights, "dp")]
    approxs = [
        inner_rows(ortho_left, right_mean, PRECISE)
        for ortho_left, right_mean in zip(orthos, right_means)
    ]
    new_errs = [matrix - approx for matrix, approx in zip(merged, approxs)]
    natural_shapes = (
        (model_width, 3, width_loc),
        (width_loc, model_width),
        (model_width, hidden_loc),
        (hidden_loc, model_width),
    )
    weights = (w_qkv, w_out, w_up, w_down)
    moments = (mom_qkv, mom_out, mom_up, mom_down)
    new_weights = []
    new_moments = []
    new_errors = []
    for weight, moment, approx, new_err, shape_now in zip(
        weights, moments, approxs, new_errs, natural_shapes
    ):
        moment_new = MOMENTUM_DECAY * moment + approx.reshape(shape_now)
        new_moments.append(moment_new)
        new_weights.append(weight - STEP_RATE * moment_new)
        new_errors.append(new_err.reshape((1,) + shape_now))
    return (
        block_out,
        input_grad,
        new_vecs[0],
        new_vecs[1],
        new_vecs[2],
        new_weights[0],
        new_weights[1],
        new_weights[2],
        new_weights[3],
        new_vec_moms[0],
        new_vec_moms[1],
        new_vec_moms[2],
        new_moments[0],
        new_moments[1],
        new_moments[2],
        new_moments[3],
        new_errors[0],
        new_errors[1],
        new_errors[2],
        new_errors[3],
        orthos[0].T[None],
        orthos[1].T[None],
        orthos[2].T[None],
        orthos[3].T[None],
        right_means[0].T[None],
        right_means[1].T[None],
        right_means[2].T[None],
        right_means[3].T[None],
    )


def solution(mesh):
    in_specs = (
        P(("dp", "tensor"), None),
        P(("dp", "tensor"), None),
        P("dp"),
        P(),
        P(),
        P(),
        P(None, None, "tensor"),
        P("tensor", None),
        P(None, "tensor"),
        P("tensor", None),
        P(),
        P(),
        P(),
        P(None, None, "tensor"),
        P("tensor", None),
        P(None, "tensor"),
        P("tensor", None),
        P("dp", None, None, "tensor"),
        P("dp", "tensor", None),
        P("dp", None, "tensor"),
        P("dp", "tensor", None),
        P("tensor", None, None),
        P("tensor", None, None),
        P("tensor", None, None),
        P("tensor", None, None),
    )
    out_specs = (
        P(("dp", "tensor"), None),
        P(("dp", "tensor"), None),
        P(),
        P(),
        P(),
        P(None, None, "tensor"),
        P("tensor", None),
        P(None, "tensor"),
        P("tensor", None),
        P(),
        P(),
        P(),
        P(None, None, "tensor"),
        P("tensor", None),
        P(None, "tensor"),
        P("tensor", None),
        P("dp", None, None, "tensor"),
        P("dp", "tensor", None),
        P("dp", None, "tensor"),
        P("dp", "tensor", None),
        P("tensor", None, None),
        P("tensor", None, None),
        P("tensor", None, None),
        P("tensor", None, None),
        P("tensor", None, None),
        P("tensor", None, None),
        P("tensor", None, None),
        P("tensor", None, None),
    )
    return jax.shard_map(shards, mesh=mesh, in_specs=in_specs, out_specs=out_specs, check_vma=False)
```

time: 2080 us -> 914 us (0.44)
  waiting for transfers between devices: 480 us -> 108 us
  other arithmetic: 392 us -> 76.2 us
  matrix products: 687 us -> 378 us
  local copies, waits for them, and re-layouts: 315 us -> 59.8 us
  Pallas kernels: 0 us -> 168 us
  loops' own time: 64.9 us -> 0 us
  between operations: 38.1 us -> 16.2 us
    dot_general x136 -> x36, matrix products: 687 us -> 378 us  [dot_on(): lax.dot_general(left_mat, right_mat, (((left_dim,), (right_dim,)), ((), (...]
    all_gather x4, waiting for transfers between devices: 335 us -> 107 us  [all_halves(): gathered = lax.all_gather(half, 'tensor', axis=axis, tiled=True)]
    reduce_sum x78 -> x2, other arithmetic: 188 us -> 7.48 us  [shards(): jnp.sum(grad_qkv.astype(jnp.float32), axis=0)]
    pallas_call x0 -> x5, Pallas kernels: none -> 168 us  [the longest x2 108 us: attention_backward(): pl.pallas_call(functools.partial(joined_backward if joined else backward_...]
    reduce_scatter x3 -> x6, waiting for transfers between devices: 145 us -> 0.02 us  [scatter(): lax.psum_scatter(grad.astype(low), 'tensor', scatter_dimension=axis, tile...]
    squeeze x57 -> x0, local copies, waits for them, and re-layouts: 75.3 us -> none  [the longest x48 66.4 us: attention_forward(): return lax.map(one_clip, (queries, key_vecs, val_vecs))]
    mul x24 -> x0, other arithmetic: 70.7 us -> none  [the longest x8 70.6 us: orthonormal(): vector * lax.rsqrt(jnp.sum(vector * vector, axis=-1, keepdims=True) + 1e-12)]
    another operation x18 -> x0, loops' own time: 64.9 us -> none  [the longest x8 32.6 us: one_clip(): lax.scan(one_block, (zero_keys, zero_keys), (offsets, clip_lse))]
  transfers between devices with their start and end apart: 7 -> 16, of which waited for: 4 -> 4; matrix products, arithmetic and copies ran while one was open for 50% -> 43% of each run, Pallas kernels for 0% -> 18%
where the time goes in v1:
time: 914 us; the launch traced here: 899 us
  matrix products  378 us (41%)
  Pallas kernels  168 us (18%)
  waiting for transfers between devices  108 us (12%)
  blocking collectives  92.2 us (10%)
  other arithmetic  76.2 us (8%)
  local copies, waits for them, and re-layouts  59.8 us (7%)
  between operations  16.2 us (2%)
    dot_general x36, matrix products, dot_on(): lax.dot_general(left_mat, right_mat, (((left_dim,), (right_dim,)), ((), (...  378 us
    pallas_call x2, Pallas kernels, attention_backward(): pl.pallas_call(functools.partial(joined_backward if joined else backward_...  108 us
    all_gather x4, waiting for transfers between devices, all_halves(): gathered = lax.all_gather(half, 'tensor', axis=axis, tiled=True)  107 us
    pallas_call x2, Pallas kernels, attention_forward(): pl.pallas_call(functools.partial(joined_forward if joined else forward_bo...  57.2 us
    psum x2, blocking collectives, psum_joined(): lax.psum(jnp.concatenate(parts, axis=1).astype(jnp.bfloat16), axis)  50.3 us
    unnamed x162, local copies, waits for them, and re-layouts  44.7 us
    psum x1, blocking collectives, shards(): lax.psum((grad_norm, grad_head_bias, grad_up_bias), ('dp', 'tensor'))  41.8 us
    convert_element_type x8, other arithmetic, scatter(): lax.psum_scatter(grad.astype(low), 'tensor', scatter_dimension=axis, tile...  21.4 us
  transfers between devices with their start and end apart: 16, of which 4 were waited for; matrix products, arithmetic and copies ran while one was open for 43% of the time, Pallas kernels for 18%

profile of v1, /device:TPU:10, one launch (start us, length us, event | category | flops | bytes accessed | tf_op | source)
XLA Modules:
  0.0 898.8 jit_solution(9570238250169544489)
XLA Ops:
  11.9 2.7 dynamic-slice_convert_fusion.1
  14.7 2.7 dynamic-slice_convert_fusion
  17.7 6.5 copy.90
  24.9 6.4 copy.94
  32.0 3.2 convert_reduce_fusion.4
  38.1 46.3 %all-gather.5.cloned.1.call-done = bf16[1024,1536]{0,1:T(8,128)(2,1)} async-done(((bf16[1024,384]{0,1:T(8,128)(2,1)}), bf16[1024,1536]{0,1:T(8,128)(2,1)}) %all-gather.5.cloned.1.call-update) | async-done | bytes 3145744 | tf_op jit(solution)/shard_map/all_gather | solution.py:286
  84.4 13.7 %add_convert_fusion.3.qkv_ref = bf16[2048,1536]{1,0:T(8,128)(2,1)} fusion(bf16[1024,1536]{0,1:T(8,128)(2,1)} %all-gather.5.cloned.1.call-done, f32[1536]{0:T(1024)S(1)} %add.274, bf16[2048,1024]{0,1:T(8,128)(2,1)} %copy.90, f32[1024]{0:T(1024)S(1)} %bitcast.234, f32[1024]{0:T(1024)S(1)} %bitcast.218, f32[2048]{0:T(1024)S(1)} %add_rsqrt_fusion.1, ...), kind=kOutput, calls=%fused_computation.17 | convolution fusion | flops 6461325312 | bytes 13662208 | tf_op jit(solution)/shard_map/dot_general | solution.py:35
  98.1 28.7 %attn_fwd.2 = (bf16[2048,512]{1,0:T(8,128)(2,1)}, f32[2048,512]{1,0:T(8,128)}) custom-call(bf16[2048,1536]{1,0:T(8,128)(2,1)} %add_convert_fusion.3.qkv_ref), custom_call_target="tpu_custom_call" | custom-call | flops 17179869184 | bytes 12582912 | tf_op jit(solution)/shard_map/attn_fwd/pallas_call | solution.py:155
  126.8 7.3 fusion.118
  134.1 5.2 all-gather.9.cloned.1.call-done
  139.3 54.9 %all-gather.11.cloned.1.call-done = bf16[2048,1024]{1,0:T(8,128)(2,1)} async-done(((bf16[512,1024]{1,0:T(8,128)(2,1)}), bf16[2048,1024]{1,0:T(8,128)(2,1)}) %all-gather.11.cloned.1.call-update) | async-done | bytes 4194320 | tf_op jit(solution)/shard_map/all_gather | solution.py:286
  194.2 13.6 %add_convert_fusion.2.qkv_ref = bf16[2048,1536]{1,0:T(8,128)(2,1)} fusion(bf16[1024,1536]{0,1:T(8,128)(2,1)} %collective-permute-done, f32[1536]{0:T(1024)S(1)} %add.278, bf16[2048,1024]{0,1:T(8,128)(2,1)} %copy.90, f32[1024]{0:T(1024)S(1)} %bitcast.235, f32[1024]{0:T(1024)S(1)} %bitcast.219, f32[2048]{0:T(1024)S(1)} %add_rsqrt_fusion.1, ...), kind=kOutput, calls=%fused_computation.16 | convolution fusion | flops 6461325312 | bytes 13662208 | tf_op jit(solution)/shard_map/dot_general | solution.py:35
  207.8 28.4 %attn_fwd.3 = (bf16[2048,512]{1,0:T(8,128)(2,1)}, f32[2048,512]{1,0:T(8,128)}) custom-call(bf16[2048,1536]{1,0:T(8,128)(2,1)} %add_convert_fusion.2.qkv_ref), custom_call_target="tpu_custom_call" | custom-call | flops 17179869184 | bytes 12582912 | tf_op jit(solution)/shard_map/attn_fwd/pallas_call | solution.py:155
  236.2 7.7 fusion.116
  249.5 25.5 %add_convert_fusion.1 = (bf16[2048,2048]{1,0:T(8,128)(2,1)}, bf16[2048,2048]{1,0:T(8,128)(2,1)}) fusion(f32[2048]{0:T(1024)S(1)} %bitcast.228, bf16[2048,1024]{0,1:T(8,128)(2,1)S(1)} %add_convert_fusion.5, bf16[1024,2048]{1,0:T(8,128)(2,1)S(1)} %copy-done.67), kind=kOutput, calls=%fused_computation.12 | convolution fusion | flops 8707375104 | bytes 25174016 | tf_op jit(solution)/shard_map/dot_general | solution.py:35
  275.0 14.6 %convert_reduce_fusion.1 = (f32[2048]{0:T(1024)}, bf16[2048,2048]{1,0:T(8,128)(2,1)}) fusion(bf16[2048,2048]{1,0:T(8,128)(2,1)} %get-tuple-element.44, bf16[2048,1024]{1,0:T(8,128)(2,1)S(1)} %copy-done.66, bf16[2048,1024]{0,1:T(8,128)(2,1)S(1)} %copy-done.5, f32[2048]{0:T(1024)S(1)} %fusion.88), kind=kOutput, calls=%fused_computation.7 | convolution fusion | flops 8617195520 | bytes 25182208 | tf_op jit(solution)/shard_map/dot_general | solution.py:35
  289.6 14.8 %fusion.120 = f32[2048,1024]{0,1:T(8,128)} fusion(bf16[2048,2048]{1,0:T(8,128)(2,1)} %get-tuple-element.216, bf16[1024,2048]{1,0:T(8,128)(2,1)} %all-gather.9.cloned.1.call-done), kind=kOutput, calls=%fused_computation.220 | convolution fusion | flops 8589934592 | bytes 20971520 | tf_op jit(solution)/shard_map/dot_general | solution.py:35
  304.4 27.9 %add_convert_fusion = (bf16[2048,2048]{1,0:T(8,128)(2,1)}, bf16[2048,2048]{1,0:T(8,128)(2,1)}) fusion(f32[2048]{0:T(1024)S(1)} %bitcast.227, bf16[2048,1024]{0,1:T(8,128)(2,1)S(1)} %add_convert_fusion.5, bf16[1024,2048]{1,0:T(8,128)(2,1)} %collective-permute-done.2), kind=kOutput, calls=%fused_computation.10 | convolution fusion | flops 8707375104 | bytes 25174016 | tf_op jit(solution)/shard_map/dot_general | solution.py:35
  332.4 15.9 %convert_reduce_fusion = (f32[2048]{0:T(1024)}, bf16[2048,2048]{1,0:T(8,128)(2,1)}) fusion(bf16[2048,2048]{1,0:T(8,128)(2,1)} %get-tuple-element.45, bf16[2048,1024]{1,0:T(8,128)(2,1)} %collective-permute-done.3, bf16[2048,1024]{0,1:T(8,128)(2,1)S(1)} %copy-done.5, f32[2048]{0:T(1024)S(1)} %fusion.88), kind=kOutput, calls=%fused_computation.6 | convolution fusion | flops 8617195520 | bytes 25182208 | tf_op jit(solution)/shard_map/dot_general | solution.py:35
  348.3 18.2 %multiply_reduce_fusion = (f32[1024]{0:T(1024)}, f32[2048]{0:T(1024)S(1)}, f32[2048]{0:T(1024)S(1)}, f32[1024]{0:T(1024)}, f32[2048,1024]{0,1:T(8,128)}) fusion(f32[2048,1024]{0,1:T(8,128)S(1)} %bitcast.193, f32[2048]{0:T(1024)S(1)} %copy-done.36, f32[2048]{0:T(1024)S(1)} %copy-done.30, f32[1024]{0:T(1024)S(1)} %bitcast.207, f32[2048,1024]{0,1:T(8,128)} %fusion.120, ...), kind=kOutput, calls=%fused_computation.39 | convolution fusion | flops 8610899968 | bytes 37793792 | tf_op jit(solution)/shard_map/dot_general | solution.py:35
  366.5 9.1 %fusion.104 = (f32[1024]{0:T(1024)}, f32[2048,1024]{0,1:T(8,128)}, f32[1024]{0:T(1024)}) fusion(f32[2048]{0:T(1024)S(1)} %broadcast_multiply_fusion.2, f32[2048,1024]{0,1:T(8,128)S(1)} %bitcast.193, f32[2048]{0:T(1024)S(1)} %copy-done.30, f32[2048]{0:T(1024)S(1)} %broadcast_multiply_fusion.3, f32[2048,1024]{0,1:T(8,128)} %get-tuple-element.211, ...), kind=kLoop, calls=%fused_computation.204 | loop fusion | flops 29358080 | bytes 29413376 | tf_op jit(solution)/shard_map/reduce_sum | solution.py:381
  375.7 4.2 convert_element_type.173
  381.8 3.4 convolution_convert_fusion.8
  385.3 6.2 convolution_convert_fusion.9
  391.5 14.0 %convolution_convert_fusion.3 = bf16[1024,2048]{1,0:T(8,128)(2,1)} fusion(bf16[2048,1024]{0,1:T(8,128)(2,1)} %copy-done.19, bf16[2048,2048]{1,0:T(8,128)(2,1)} %get-tuple-element.216), kind=kOutput, calls=%fused_computation.80 | convolution fusion | flops 8592031744 | bytes 16777216 | tf_op jit(solution)/shard_map/dot_general | solution.py:35
  405.6 14.1 %convolution_convert_fusion.5 = bf16[2048,1024]{1,0:T(8,128)(2,1)} fusion(bf16[2048,2048]{1,0:T(8,128)(2,1)} %get-tuple-element.42, bf16[2048,1024]{0,1:T(8,128)(2,1)} %copy.94, f32[2048]{0:T(1024)S(1)} %fusion.88), kind=kOutput, calls=%fused_computation.82 | convolution fusion | flops 8598323200 | bytes 16785408 | tf_op jit(solution)/shard_map/dot_general | solution.py:35
  420.9 5.9 convolution_convert_fusion.6.do_ref
  426.9 54.1 %attn_bwd.3 = bf16[2048,1536]{1,0:T(8,128)(2,1)} custom-call(bf16[2048,1536]{1,0:T(8,128)(2,1)} %add_convert_fusion.2.qkv_ref, bf16[2048,512]{1,0:T(8,128)(2,1)} %get-tuple-element.41.ctx_ref, f32[2048,512]{1,0:T(8,128)} %get-tuple-element.47.lse_ref, bf16[2048,512]{1,0:T(8,128)(2,1)} %convolution_convert_fusion.6.do_ref), custom_call_target="tpu_custom_call" | custom-call | flops 42949672960 | bytes 20971520 | tf_op jit(solution)/shard_map/attn_bwd/pallas_call | solution.py:189
  481.0 10.6 %convolution_convert_fusion = bf16[1024,1536]{1,0:T(8,128)(2,1)S(1)} fusion(bf16[2048,1536]{1,0:T(8,128)(2,1)} %attn_bwd.3, bf16[2048,1024]{0,1:T(8,128)(2,1)} %copy.90, f32[1024]{0:T(1024)S(1)} %bitcast.236, f32[1024]{0:T(1024)S(1)} %bitcast.220, f32[2048]{0:T(1024)S(1)} %copy-done.42, f32[2048]{0:T(1024)S(1)} %copy-done.34), kind=kOutput, calls=%fused_computation.77 | convolution fusion | flops 6456606720 | bytes 13656064 | tf_op jit(solution)/shard_map/dot_general | solution.py:35
  491.7 2.9 copy.115
  494.6 6.2 convolution_convert_fusion.7.do_ref
  500.8 53.8 %attn_bwd.2 = bf16[2048,1536]{1,0:T(8,128)(2,1)} custom-call(bf16[2048,1536]{1,0:T(8,128)(2,1)} %add_convert_fusion.3.qkv_ref, bf16[2048,512]{1,0:T(8,128)(2,1)} %get-tuple-element.40.ctx_ref, f32[2048,512]{1,0:T(8,128)} %get-tuple-element.46.lse_ref, bf16[2048,512]{1,0:T(8,128)(2,1)} %convolution_convert_fusion.7.do_ref), custom_call_target="tpu_custom_call" | custom-call | flops 42949672960 | bytes 20971520 | tf_op jit(solution)/shard_map/attn_bwd/pallas_call | solution.py:189
  554.7 10.7 %convolution_convert_fusion.1 = bf16[1024,1536]{1,0:T(8,128)(2,1)S(1)} fusion(bf16[2048,1536]{1,0:T(8,128)(2,1)} %attn_bwd.2, bf16[2048,1024]{0,1:T(8,128)(2,1)} %copy.90, f32[1024]{0:T(1024)S(1)} %bitcast.237, f32[1024]{0:T(1024)S(1)} %bitcast.221, f32[2048]{0:T(1024)S(1)} %copy-done.42, f32[2048]{0:T(1024)S(1)} %copy-done.34), kind=kOutput, calls=%fused_computation.78 | convolution fusion | flops 6456606720 | bytes 13656064 | tf_op jit(solution)/shard_map/dot_general | solution.py:35
  565.4 2.9 copy.113
  570.7 14.0 %convolution_convert_fusion.2 = bf16[1024,2048]{1,0:T(8,128)(2,1)} fusion(bf16[2048,1024]{0,1:T(8,128)(2,1)} %copy-done.19, bf16[2048,2048]{1,0:T(8,128)(2,1)} %get-tuple-element.214), kind=kOutput, calls=%fused_computation.79 | convolution fusion | flops 8592031744 | bytes 16777216 | tf_op jit(solution)/shard_map/dot_general | solution.py:35
  584.8 15.0 %fusion.119 = f32[2048,1024]{0,1:T(8,128)} fusion(bf16[2048,2048]{1,0:T(8,128)(2,1)} %get-tuple-element.42, bf16[2048,1024]{1,0:T(8,128)(2,1)} %all-gather.11.cloned.1.call-done), kind=kOutput, calls=%fused_computation.219 | convolution fusion | flops 8589934592 | bytes 20971520 | tf_op jit(solution)/shard_map/dot_general | solution.py:35
  599.9 3.8 convert_reduce_fusion.2
  603.6 12.0 %fusion.121 = f32[2048,1024]{0,1:T(8,128)} fusion(bf16[2048,1536]{1,0:T(8,128)(2,1)} %attn_bwd.2, bf16[1024,1536]{0,1:T(8,128)(2,1)} %all-gather.5.cloned.1.call-done), kind=kOutput, calls=%fused_computation.221 | convolution fusion | flops 6442450944 | bytes 17825792 | tf_op jit(solution)/shard_map/dot_general | solution.py:35
  615.7 16.8 %fusion.15 = (f32[1024]{0:T(1024)S(1)}, f32[2048]{0:T(1024)S(1)}, f32[2048]{0:T(1024)S(1)}, f32[1024]{0:T(1024)S(1)}, f32[2048,1024]{0,1:T(8,128)}) fusion(bf16[2048,1024]{0,1:T(8,128)(2,1)S(1)} %copy-done.3, f32[2048]{0:T(1024)S(1)} %copy-done.42, f32[2048]{0:T(1024)S(1)} %copy-done.34, f32[1024]{0:T(1024)S(1)} %bitcast.222, f32[2048,1024]{0,1:T(8,128)} %fusion.121, ...), kind=kOutput, calls=%fused_computation.36 | convolution fusion | flops 6465513472 | bytes 30453760 | tf_op jit(solution)/shard_map/dot_general | solution.py:35
  632.5 14.0 %convolution_convert_fusion.4 = bf16[2048,1024]{1,0:T(8,128)(2,1)} fusion(bf16[2048,2048]{1,0:T(8,128)(2,1)} %get-tuple-element.43, bf16[2048,1024]{0,1:T(8,128)(2,1)} %copy.94, f32[2048]{0:T(1024)S(1)} %copy-done.49), kind=kOutput, calls=%fused_computation.81 | convolution fusion | flops 8598323200 | bytes 16785408 | tf_op jit(solution)/shard_map/dot_general | solution.py:35
  646.5 10.9 %fusion.14 = bf16[2048,1024]{0,1:T(8,128)(2,1)} fusion(f32[2048,1024]{0,1:T(8,128)} %get-tuple-element.162, bf16[2048,1024]{0,1:T(8,128)(2,1)} %copy.90, f32[2048,1024]{0,1:T(8,128)} %get-tuple-element.212, f32[2048]{0:T(1024)S(1)} %broadcast_multiply_fusion, f32[2048]{0:T(1024)S(1)} %broadcast_multiply_fusion.1, f32[1024]{0:T(1024)S(1)} %bitcast.223, ...), kind=kLoop, calls=%fused_computation.35 | loop fusion | flops 20971520 | bytes 25202688 | tf_op jit(solution)/shard_map/convert_element_type | solution.py:410
  657.5 3.7 convert_reduce_fusion.3
  661.2 6.8 copy.105
  668.0 18.5 %add_convert_fusion.4 = bf16[2048,1024]{0,1:T(8,128)(2,1)} fusion(f32[2048,1024]{0,1:T(8,128)} %copy-done.1, f32[2048,1024]{0,1:T(8,128)} %fusion.119, f32[1024]{0:T(1024)S(1)} %bitcast.233, bf16[2048,2048]{1,0:T(8,128)(2,1)} %get-tuple-element.43, bf16[2048,1024]{1,0:T(8,128)(2,1)} %collective-permute-done.3), kind=kOutput, calls=%fused_computation.42 | convolution fusion | flops 8598323200 | bytes 33558528 | tf_op jit(solution)/shard_map/dot_general | solution.py:35
  686.7 6.5 copy.104
  693.3 41.8 %all-reduce = (f32[6,1024]{1,0:T(8,128)S(1)}, f32[2,1024]{1,0:T(2,128)S(1)}, f32[4096]{0:T(1024)S(1)}) all-reduce(f32[6,1024]{1,0:T(8,128)S(1)} %stack.42, f32[2,1024]{1,0:T(2,128)S(1)} %pad_maximum_fusion.4, f32[4096]{0:T(1024)S(1)} %bitcast.205), channel_id=1, replica_groups=mesh['dp'=8,'tensor'=4] {'dp','tensor'}, use_global_device_ids=true, to_apply=%region_14.15 | all-reduce | flops 12288 | bytes 98304 | tf_op jit(solution)/shard_map/psum | solution.py:423
  743.5 3.8 fusion.105
  747.3 3.9 fusion.107
  762.4 3.0 fusion.106
  765.4 6.2 fusion.48
  771.6 3.0 fusion.108
  774.6 5.7 fusion.51
  780.4 23.9 %psum.38 = bf16[8,3328]{1,0:T(8,128)(2,1)S(1)} all-reduce(bf16[8,3328]{1,0:T(8,128)(2,1)S(1)} %pad_maximum_fusion.1), channel_id=1, replica_groups=mesh['dp'=8,'tensor'=4] {'dp'}, use_global_device_ids=true, to_apply=%region_29.30 | all-reduce | flops 26624 | bytes 106496 | tf_op jit(solution)/shard_map/psum | solution.py:232
  805.6 2.8 orthonormal.1
  808.4 3.5 convolution_convert_fusion.14
  812.0 2.7 convolution_convert_fusion.12
  814.7 4.4 convolution_convert_fusion.11
  821.9 26.4 %psum.39 = bf16[8,3840]{1,0:T(8,128)(2,1)S(1)} all-reduce(bf16[8,3840]{1,0:T(8,128)(2,1)S(1)} %pad_maximum_fusion), channel_id=1, replica_groups=mesh['dp'=8,'tensor'=4] {'dp'}, use_global_device_ids=true, to_apply=%region_30.31 | all-reduce | flops 30720 | bytes 122880 | tf_op jit(solution)/shard_map/psum | solution.py:232
  848.3 4.6 fusion.117
  854.2 10.0 %multiply_subtract_fusion = (f32[1024,1024]{1,0:T(8,128)}, f32[1024,1024]{1,0:T(8,128)}, f32[1,1024,1024]{2,1,0:T(8,128)}) fusion(f32[1024,1024]{1,0:T(8,128)S(1)} %copy-done.16, f32[1024,1024]{1,0:T(8,128)} %param.41, f32[1,1024,1024]{2,1,0:T(8,128)} %param.45, f32[512,1024]{1,0:T(8,128)S(1)} %copy-done.11, f32[512,1024]{1,0:T(8,128)S(1)} %copy-done.15, ...), kind=kOutput, calls=%fused_computation.72 | convolution fusion | flops 110108672 | bytes 29425664 | tf_op jit(solution)/shard_map/dot_general | solution.py:35
  864.4 10.7 %multiply_subtract_fusion.1 = (f32[1024,1024]{1,0:T(8,128)}, f32[1024,1024]{1,0:T(8,128)}, f32[1,1024,1024]{2,1,0:T(8,128)}) fusion(f32[1024,1024]{1,0:T(8,128)S(1)} %copy-done.17, f32[1024,1024]{1,0:T(8,128)} %param.40, f32[1,1024,1024]{2,1,0:T(8,128)} %param.44, f32[1024,512]{1,0:T(8,128)S(1)} %copy-done.9, f32[1024,512]{1,0:T(8,128)S(1)} %copy-done.13, ...), kind=kOutput, calls=%fused_computation.74 | convolution fusion | flops 110108672 | bytes 29425664 | tf_op jit(solution)/shard_map/dot_general | solution.py:35
  875.2 3.0 multiply_subtract_fusion.3
  878.2 3.7 copy.103
  884.2 7.4 multiply_subtract_fusion.2
  (250 shorter events, 47.6 us)
Async XLA Ops:
  7.2 758.2 %copy-start = (f32[1,1024,8]{1,2,0:T(8,128)S(1)}, f32[1,1024,8]{1,2,0:T(8,128)}, u32[]{:S(2)}) copy-start(f32[1,1024,8]{1,2,0:T(8,128)} %param.48) | copy-start | bytes 98308
  7.2 30.9 %all-gather.7.cloned.1.call-start = ((), (), s32[]{:S(2)}) async-start(), calls=%async_computation.9 | async-start | bytes 1310720 | tf_op jit(solution)/shard_map/all_gather | solution.py:286
  9.1 75.3 %all-gather.5.cloned.1.call-start = ((), (), s32[]{:S(2)}) async-start(), calls=%async_computation.8 | async-start | bytes 3932160 | tf_op jit(solution)/shard_map/all_gather | solution.py:286
  10.7 6.8 copy-start.44
  11.9 127.4 %all-gather.9.cloned.1.call-start = ((), (), s32[]{:S(2)}) async-start(), calls=%async_computation.10 | async-start | bytes 5242880 | tf_op jit(solution)/shard_map/all_gather | solution.py:286
  14.6 179.5 %all-gather.11.cloned.1.call-start = ((), (), s32[]{:S(2)}) async-start(), calls=%async_computation.11 | async-start | bytes 5242880 | tf_op jit(solution)/shard_map/all_gather | solution.py:286
  17.4 719.7 %reduce-scatter.15.cloned.1.call-start = ((), (), s32[]{:S(2)}) async-start(), calls=%async_computation.13 | async-start | bytes 1310720 | tf_op jit(solution)/shard_map/reduce_scatter | solution.py:363
  31.3 374.3 %copy-start.48 = (f32[2048]{0:T(1024)}, f32[2048]{0:T(1024)S(1)}, u32[]{:S(2)}) copy-start(f32[2048]{0:T(1024)S(1)} %fusion.88) | copy-start | bytes 24580
  35.1 159.0 %copy-start.33 = (f32[2048]{0:T(1024)}, f32[2048]{0:T(1024)S(1)}, u32[]{:S(2)}) copy-start(f32[2048]{0:T(1024)S(1)} %broadcast_multiply_fusion.5) | copy-start | bytes 24580
  36.3 157.9 %copy-start.41 = (f32[2048]{0:T(1024)}, f32[2048]{0:T(1024)S(1)}, u32[]{:S(2)}) copy-start(f32[2048]{0:T(1024)S(1)} %add_rsqrt_fusion.1) | copy-start | bytes 24580
  36.9 157.2 %copy-start.54 = (f32[1,1024]{1,0:T(1,128)}, f32[1,1024]{1,0:T(1,128)S(1)}, u32[]{:S(2)}) copy-start(f32[1,1024]{1,0:T(1,128)S(1)} %get-tuple-element.194) | copy-start | bytes 12292
  36.9 157.3 %copy-start.64 = (f32[1,1024]{1,0:T(1,128)}, f32[1,1024]{1,0:T(1,128)S(1)}, u32[]{:S(2)}) copy-start(f32[1,1024]{1,0:T(1,128)S(1)} %get-tuple-element.193) | copy-start | bytes 12292
  36.9 207.9 %copy-start.39 = (f32[1,1024]{1,0:T(1,128)}, f32[1,1024]{1,0:T(1,128)S(1)}, u32[]{:S(2)}) copy-start(f32[1,1024]{1,0:T(1,128)S(1)} %get-tuple-element.191) | copy-start | bytes 12292
  38.1 198.1 %collective-permute-start.1 = (bf16[512,1024]{1,0:T(8,128)(2,1)}, bf16[512,1024]{1,0:T(8,128)(2,1)S(1)}, u32[]{:S(2)}, u32[]{:S(2)}) collective-permute-start(bf16[512,1024]{1,0:T(8,128)(2,1)} %all-gather.7.cloned.1.call-done), channel_id=1, source_target_pairs={{0,4},{4,0},{8,12},{12,8},{16,20},{20,16},{24,28},{28,24},{1,5},{5... | collective-permute-start | bytes 3145736 | tf_op jit(solution)/shard_map/ppermute | solution.py:290
  84.4 109.8 %collective-permute-start = (bf16[1024,1536]{0,1:T(8,128)(2,1)}, bf16[1024,1536]{0,1:T(8,128)(2,1)}, u32[]{:S(2)}, u32[]{:S(2)}) collective-permute-start(bf16[1024,1536]{0,1:T(8,128)(2,1)} %all-gather.5.cloned.1.call-done), channel_id=1, source_target_pairs={{0,4},{4,0},{8,12},{12,8},{16,20},{20,16},{24,28},{28,24},{1,5},{5... | collective-permute-start | bytes 9437192 | tf_op jit(solution)/shard_map/ppermute | solution.py:290
  98.1 28.7 %copy-start.68 = (bf16[512,1024]{1,0:T(8,128)(2,1)S(1)}, bf16[512,1024]{1,0:T(8,128)(2,1)}, u32[]{:S(2)}) copy-start(bf16[512,1024]{1,0:T(8,128)(2,1)} %all-gather.7.cloned.1.call-done) | copy-start | bytes 3145732
  139.3 165.1 %collective-permute-start.2 = (bf16[1024,2048]{1,0:T(8,128)(2,1)}, bf16[1024,2048]{1,0:T(8,128)(2,1)}, u32[]{:S(2)}, u32[]{:S(2)}) collective-permute-start(bf16[1024,2048]{1,0:T(8,128)(2,1)} %all-gather.9.cloned.1.call-done), channel_id=1, source_target_pairs={{0,4},{4,0},{8,12},{12,8},{16,20},{20,16},{24,28},{28,24},{1,5},{5... | collective-permute-start | bytes 12582920 | tf_op jit(solution)/shard_map/ppermute | solution.py:290
  194.2 138.2 %collective-permute-start.3 = (bf16[2048,1024]{1,0:T(8,128)(2,1)}, bf16[2048,1024]{1,0:T(8,128)(2,1)}, u32[]{:S(2)}, u32[]{:S(2)}) collective-permute-start(bf16[2048,1024]{1,0:T(8,128)(2,1)} %all-gather.11.cloned.1.call-done), channel_id=1, source_target_pairs={{0,4},{4,0},{8,12},{12,8},{16,20},{20,16},{24,28},{28,24},{1,5},{5... | collective-permute-start | bytes 12582920 | tf_op jit(solution)/shard_map/ppermute | solution.py:290
  236.2 7.7 copy-start.69
  248.9 55.6 %copy-start.19 = (bf16[2048,1024]{0,1:T(8,128)(2,1)}, bf16[2048,1024]{0,1:T(8,128)(2,1)S(1)}, u32[]{:S(2)}) copy-start(bf16[2048,1024]{0,1:T(8,128)(2,1)S(1)} %add_convert_fusion.5) | copy-start | bytes 12582916
  249.5 25.6 %copy-start.5 = (bf16[2048,1024]{0,1:T(8,128)(2,1)S(1)}, bf16[2048,1024]{0,1:T(8,128)(2,1)}, u32[]{:S(2)}) copy-start(bf16[2048,1024]{0,1:T(8,128)(2,1)} %copy.94) | copy-start | bytes 12582916
  249.5 25.6 %copy-start.66 = (bf16[2048,1024]{1,0:T(8,128)(2,1)S(1)}, bf16[2048,1024]{1,0:T(8,128)(2,1)}, u32[]{:S(2)}) copy-start(bf16[2048,1024]{1,0:T(8,128)(2,1)} %all-gather.11.cloned.1.call-done) | copy-start | bytes 12582916
  289.6 14.8 %copy-start.60 = (f32[4,1,512]{2,1,0:T(1,128)S(1)}, f32[4,1,512]{2,1,0:T(1,128)}, u32[]{:S(2)}) copy-start(f32[4,1,512]{2,1,0:T(1,128)} %get-tuple-element.195) | copy-start | bytes 24580
  332.3 15.9 %slice-start = ((s8[8388608]{0:T(1024)(128)(4,1)}), s8[4194304]{0:T(1024)(128)(4,1)S(1)}, s32[]{:S(2)}) async-start(s8[8388608]{0:T(1024)(128)(4,1)} %bitcast.192), calls=%async_computation.20 | async-start | bytes 8388608
  332.3 15.9 %slice-start.1 = ((s8[8388608]{0:T(1024)(128)(4,1)}), s8[4194304]{0:T(1024)(128)(4,1)S(1)}, s32[]{:S(2)}) async-start(s8[8388608]{0:T(1024)(128)(4,1)} %bitcast.192), calls=%async_computation.21 | async-start | bytes 8388608
  332.3 15.9 %copy-start.30 = (f32[2048]{0:T(1024)S(1)}, f32[2048]{0:T(1024)}, u32[]{:S(2)}) copy-start(f32[2048]{0:T(1024)} %copy-done.29) | copy-start | bytes 24580
  332.3 15.9 %copy-start.36 = (f32[2048]{0:T(1024)S(1)}, f32[2048]{0:T(1024)}, u32[]{:S(2)}) copy-start(f32[2048]{0:T(1024)} %copy-done.35) | copy-start | bytes 24580
  332.4 15.9 %copy-start.40 = (f32[1,1024]{1,0:T(1,128)S(1)}, f32[1,1024]{1,0:T(1,128)}, u32[]{:S(2)}) copy-start(f32[1,1024]{1,0:T(1,128)} %copy-done.39) | copy-start | bytes 12292
  385.2 353.9 %reduce-scatter.13.cloned.1.call-start = ((), (), s32[]{:S(2)}) async-start(), calls=%async_computation.12 | async-start | bytes 1310720 | tf_op jit(solution)/shard_map/reduce_scatter | solution.py:363
  391.5 352.0 %reduce-scatter.17.cloned.1.call-start = ((), (), s32[]{:S(2)}) async-start(), calls=%async_computation.14 | async-start | bytes 5242880 | tf_op jit(solution)/shard_map/reduce_scatter | solution.py:363
  405.6 341.8 %reduce-scatter.21.cloned.1.call-start = ((), (), s32[]{:S(2)}) async-start(), calls=%async_computation.16 | async-start | bytes 5242880 | tf_op jit(solution)/shard_map/reduce_scatter | solution.py:363
  419.7 331.4 %reduce-scatter.27.cloned.1.call-start = ((), (), s32[]{:S(2)}) async-start(), calls=%async_computation.19 | async-start | bytes 3932160
  426.8 54.2 %copy-start.34 = (f32[2048]{0:T(1024)S(1)}, f32[2048]{0:T(1024)}, u32[]{:S(2)}) copy-start(f32[2048]{0:T(1024)} %copy-done.33) | copy-start | bytes 24580
  426.9 54.2 %copy-start.42 = (f32[2048]{0:T(1024)S(1)}, f32[2048]{0:T(1024)}, u32[]{:S(2)}) copy-start(f32[2048]{0:T(1024)} %copy-done.41) | copy-start | bytes 24580
  426.9 54.2 %copy-start.55 = (f32[1,1024]{1,0:T(1,128)S(1)}, f32[1,1024]{1,0:T(1,128)}, u32[]{:S(2)}) copy-start(f32[1,1024]{1,0:T(1,128)} %copy-done.54) | copy-start | bytes 12292
  426.9 54.2 %copy-start.65 = (f32[1,1024]{1,0:T(1,128)S(1)}, f32[1,1024]{1,0:T(1,128)}, u32[]{:S(2)}) copy-start(f32[1,1024]{1,0:T(1,128)} %copy-done.64) | copy-start | bytes 12292
  494.6 259.1 %reduce-scatter.25.cloned.1.call-start = ((), (), s32[]{:S(2)}) async-start(), calls=%async_computation.18 | async-start | bytes 3932160
  568.3 194.1 %reduce-scatter.19.cloned.1.call-start = ((), (), s32[]{:S(2)}) async-start(), calls=%async_computation.15 | async-start | bytes 5242880 | tf_op jit(solution)/shard_map/reduce_scatter | solution.py:363
  584.7 15.1 %copy-start.58 = (f32[2048]{0:T(1024)S(1)}, f32[2048]{0:T(1024)}, u32[]{:S(2)}) copy-start(f32[2048]{0:T(1024)} %get-tuple-element.215) | copy-start | bytes 24580
  584.8 15.1 %copy-start.59 = (f32[2048]{0:T(1024)S(1)}, f32[2048]{0:T(1024)}, u32[]{:S(2)}) copy-start(f32[2048]{0:T(1024)} %get-tuple-element.213) | copy-start | bytes 24580
  584.8 186.9 %reduce-scatter.23.cloned.1.call-start = ((), (), s32[]{:S(2)}) async-start(), calls=%async_computation.17 | async-start | bytes 5242880 | tf_op jit(solution)/shard_map/reduce_scatter | solution.py:363
  603.6 12.0 %copy-start.3 = (bf16[2048,1024]{0,1:T(8,128)(2,1)S(1)}, bf16[2048,1024]{0,1:T(8,128)(2,1)}, u32[]{:S(2)}) copy-start(bf16[2048,1024]{0,1:T(8,128)(2,1)} %copy.90) | copy-start | bytes 12582916
  615.7 16.8 %copy-start.49 = (f32[2048]{0:T(1024)S(1)}, f32[2048]{0:T(1024)}, u32[]{:S(2)}) copy-start(f32[2048]{0:T(1024)} %copy-done.48) | copy-start | bytes 24580
  661.2 6.8 copy-start.63
  686.6 6.6 copy-start.52
  686.6 6.6 copy-start.61
  686.6 48.6 %copy-start.45 = (f32[2,1024]{1,0:T(2,128)S(1)}, f32[2,1024]{1,0:T(2,128)}, u32[]{:S(2)}) copy-start(f32[2,1024]{1,0:T(2,128)} %param.29) | copy-start | bytes 24580
  686.6 48.6 %copy-start.57 = (f32[2,1024]{1,0:T(2,128)S(1)}, f32[2,1024]{1,0:T(2,128)}, u32[]{:S(2)}) copy-start(f32[2,1024]{1,0:T(2,128)} %param.36) | copy-start | bytes 24580
  686.6 49.2 %copy-start.38 = (f32[4096]{0:T(1024)S(1)}, f32[4096]{0:T(1024)}, u32[]{:S(2)}) copy-start(f32[4096]{0:T(1024)} %param.30) | copy-start | bytes 49156
  686.6 49.2 %copy-start.53 = (f32[4096]{0:T(1024)S(1)}, f32[4096]{0:T(1024)}, u32[]{:S(2)}) copy-start(f32[4096]{0:T(1024)} %param.37) | copy-start | bytes 49156
  686.6 49.8 %copy-start.32 = (f32[6,1024]{1,0:T(8,128)S(1)}, f32[6,1024]{1,0:T(8,128)}, u32[]{:S(2)}) copy-start(f32[6,1024]{1,0:T(8,128)} %param.28) | copy-start | bytes 73732
  686.6 49.8 %copy-start.43 = (f32[6,1024]{1,0:T(8,128)S(1)}, f32[6,1024]{1,0:T(8,128)}, u32[]{:S(2)}) copy-start(f32[6,1024]{1,0:T(8,128)} %param.35) | copy-start | bytes 73732
  686.7 54.4 %copy-start.71 = (f32[1,1024,8]{1,2,0:T(8,128)S(1)}, f32[1,1024,8]{1,2,0:T(8,128)}, u32[]{:S(2)}) copy-start(f32[1,1024,8]{1,2,0:T(8,128)} %param.47) | copy-start | bytes 98308
  774.6 33.8 %copy-start.4 = (f32[1024,768]{0,1:T(8,128)S(1)}, f32[1024,768]{0,1:T(8,128)}, u32[]{:S(2)}) copy-start(f32[1024,768]{0,1:T(8,128)} %bitcast_add_fusion) | copy-start | bytes 9437188
  819.4 28.9 %copy-start.28 = (f32[8,1024]{1,0:T(8,128)S(1)}, f32[8,1024]{1,0:T(8,128)}, u32[]{:S(2)}) copy-start(f32[8,1024]{1,0:T(8,128)} %get-tuple-element.48) | copy-start | bytes 98308
  854.2 10.1 %copy-start.9 = (f32[1024,512]{1,0:T(8,128)S(1)}, f32[1024,512]{1,0:T(8,128)}, u32[]{:S(2)}) copy-start(f32[1024,512]{1,0:T(8,128)} %get-tuple-element.171) | copy-start | bytes 6291460
  854.2 10.1 %copy-start.13 = (f32[1024,512]{1,0:T(8,128)S(1)}, f32[1024,512]{1,0:T(8,128)}, u32[]{:S(2)}) copy-start(f32[1024,512]{1,0:T(8,128)} %get-tuple-element.173) | copy-start | bytes 6291460
  854.2 10.1 %copy-start.17 = (f32[1024,1024]{1,0:T(8,128)S(1)}, f32[1024,1024]{1,0:T(8,128)}, u32[]{:S(2)}) copy-start(f32[1024,1024]{1,0:T(8,128)} %param.33) | copy-start | bytes 12582916
  864.3 10.8 %copy-start.23 = (f32[128,1024]{1,0:T(8,128)S(1)}, f32[128,1024]{1,0:T(8,128)}, u32[]{:S(2)}) copy-start(f32[128,1024]{1,0:T(8,128)} %get-tuple-element.181) | copy-start | bytes 1572868
  864.3 10.8 %copy-start.24 = (f32[128,1024]{1,0:T(8,128)S(1)}, f32[128,1024]{1,0:T(8,128)}, u32[]{:S(2)}) copy-start(f32[128,1024]{1,0:T(8,128)} %get-tuple-element.179) | copy-start | bytes 1572868
  864.3 10.8 %copy-start.25 = (f32[256,1024]{1,0:T(8,128)S(1)}, f32[256,1024]{1,0:T(8,128)}, u32[]{:S(2)}) copy-start(f32[256,1024]{1,0:T(8,128)} %param.32) | copy-start | bytes 3145732
  864.3 10.8 %copy-start.26 = (f32[1,256,1024]{2,1,0:T(8,128)S(1)}, f32[1,256,1024]{2,1,0:T(8,128)}, u32[]{:S(2)}) copy-start(f32[1,256,1024]{2,1,0:T(8,128)} %param.43) | copy-start | bytes 3145732
  864.3 10.8 %copy-start.27 = (f32[256,1024]{1,0:T(8,128)S(1)}, f32[256,1024]{1,0:T(8,128)}, u32[]{:S(2)}) copy-start(f32[256,1024]{1,0:T(8,128)} %param.39) | copy-start | bytes 3145732
  864.4 10.8 %copy-start.56 = (f32[8,256]{1,0:T(8,128)S(1)}, f32[8,256]{1,0:T(8,128)}, u32[]{:S(2)}) copy-start(f32[8,256]{1,0:T(8,128)} %get-tuple-element.49) | copy-start | bytes 24580
  (28 other events, 122.4 us)
Sparse Core Ops, SparseCore 0:
  10.4 27.6 all-gather.6
  40.5 43.8 all-gather.4
  86.8 52.4 all-gather.8
  141.6 52.5 all-gather.10
  385.3 28.0 reduce-scatter.14
  416.8 27.9 reduce-scatter.12
  447.7 52.5 reduce-scatter.16
  503.9 52.5 reduce-scatter.20
  560.1 43.8 reduce-scatter.26
  607.4 43.8 reduce-scatter.24
  654.9 53.0 reduce-scatter.18
  711.4 53.3 reduce-scatter.22
